TPU v7x, 32 devices: a whole 2x2x4 slice. The times are simulated.
32 devices in a mesh: fs: 8 (over z, x), pol: 4 (over y, core).
Axes of the slice: x: 2, y: 2, z: 4, core: 2. Of those that a mesh axis runs over, the one named last changes fastest.
Arguments:
- facets: bfloat16 [4, 64, 4096, 128], P('pol', 'fs'), may hold values from -6 to 6
- owners: int32 [64], replicated, may hold values from 0 to 7, as said below
- counts: int32 [64], replicated, may hold values from 1 to 8, as said below
- coords: float32 [2, 128, 8, 128], P(None, 'fs'), may hold values from 0 to 512
- station_ids: int32 [128, 8, 2, 128], P('fs'), may hold values from 0 to 511
- jones_table: float32 [8, 512], replicated, may hold values from -3 to 3
Outputs:
- predicted: float32 [4, 2, 128, 8, 128], P('pol', None, 'fs')
Inputs may be any that keep to these rules, and one draw needn't show every extreme that they name: `owners`: each fs index owns at most 16 subgrids, and some index owns exactly 16. `counts`: some subgrid has exactly 8 blocks.
All inputs are finite; a program needn't handle non-finite values.
Results may differ from a plain program's by a relative error of at most 0.0055.
Values may be sent and summed in bfloat16 or wider, within the bound.
A program may use at most 128 MiB of HBM per device.

v0:
```python
import functools
import math

import jax
import jax.numpy as jnp
from jax import lax
from jax.experimental import pallas as pl
from jax.experimental.pallas import tpu as pltpu
from jax.sharding import PartitionSpec as P

R = 8
W = 64
S = 64
FH = 4096
SG = 512
UNROLL = 4
GROUP = 4

SIN_COEFS = [
    (-1) ** i * math.pi ** (2 * i + 1) / math.factorial(2 * i + 1) for i in range(6)
]
COS_COEFS = [(-1) ** i * math.pi ** (2 * i) / math.factorial(2 * i) for i in range(7)]


def dft_tables(length):
    indices = jnp.arange(length, dtype=jnp.int32)
    phases = indices[:, None] * indices[None, :] % length
    angles = phases.astype(jnp.float32) * (2.0 * math.pi / length)
    return (jnp.cos(angles).astype(jnp.bfloat16), jnp.sin(angles).astype(jnp.bfloat16))


def turn_table(rows, cols, length):
    row_index = jnp.arange(rows, dtype=jnp.int32)
    col_index = jnp.arange(cols, dtype=jnp.int32)
    phases = row_index[:, None] * col_index[None, :] % length
    angles = phases.astype(jnp.float32) * (2.0 * math.pi / length)
    return (jnp.cos(angles), jnp.sin(angles))


def horner(coefs, square):
    total = jnp.full_like(square, coefs[-1])
    for coef in coefs[-2::-1]:
        total = total * square + coef
    return total


def phase(position, multiple):
    halves = position * (multiple * (2.0 / SG))
    nearest = jnp.floor(halves + 0.5)
    rest = halves - nearest
    square = rest * rest
    pairs = nearest * 0.5
    flip = 1.0 - 4.0 * (pairs - jnp.floor(pairs))
    return horner(COS_COEFS, square) * flip, horner(SIN_COEFS, square) * (rest * flip)


def twice(left, right):
    return (left[0] * right[0] - left[1] * right[1], left[1] * right[0] + left[0] * right[1])


def turn_lanes(values, sign):
    return pltpu.roll(values, W, 1) * sign


def transform_kernel(
    device_count, first_ref, second_ref, turn_cos_ref, turn_sin_ref, coords_ref, strip_ref, out_ref,
    gathered_ref, turned_ref, window_ref, everyone_ref, own_sem, send_sem, recv_sem
):
    me = lax.axis_index("fs")
    copies = [
        pltpu.make_async_remote_copy(
            src_ref=everyone_ref.at[me],
            dst_ref=everyone_ref.at[me],
            send_sem=send_sem.at[step],
            recv_sem=recv_sem.at[step],
            device_id={"fs": lax.rem(me + step + 1, device_count)},
            device_id_type=pl.DeviceIdType.MESH,
        )
        for step in range(device_count - 1)
    ]

    @pl.when(pl.program_id(0) == 0)
    def _():
        own = pltpu.make_async_copy(coords_ref, everyone_ref.at[me], own_sem)
        own.start()
        barrier = pltpu.get_barrier_semaphore()
        for step in range(device_count - 1):
            pl.semaphore_signal(
                barrier,
                inc=1,
                device_id={"fs": lax.rem(me + step + 1, device_count)},
                device_id_type=pl.DeviceIdType.MESH,
            )
        pl.semaphore_wait(barrier, device_count - 1)
        own.wait()
        for copy in copies:
            copy.start()

    width = 2 * W
    lanes = lax.broadcasted_iota(jnp.int32, (1, width), 1)
    sign = jnp.where(lanes < W, 1.0, -1.0)

    def first(i, carry):
        start = pl.multiple_of(i * 16, 16)
        strips = jnp.swapaxes(strip_ref[0, :, pl.ds(start, 16), :].astype(jnp.float32), 0, 1)
        strips = strips.astype(jnp.bfloat16)
        for j in range(0, 16, GROUP):
            data = jnp.concatenate([strips[j + u] for u in range(GROUP)], axis=1)
            both = jnp.dot(first_ref[...], data, preferred_element_type=jnp.float32)
            for u in range(GROUP):
                n = start + j + u
                part = both[:, u * width : (u + 1) * width]
                tc, ts = turn_cos_ref[n], turn_sin_ref[n]
                straight = part[:W] * tc - part[W:] * ts
                crossed = part[W:] * tc + part[:W] * ts
                turned_ref[n] = straight + turn_lanes(crossed, sign)
        return carry

    lax.fori_loop(0, S // 16, first, 0)

    def second(i, carry):
        start = pl.multiple_of(i * 8, 8)
        turned = jnp.swapaxes(turned_ref[:, pl.ds(start, 8), :], 0, 1).astype(jnp.bfloat16)
        for j in range(0, 8, GROUP):
            data = jnp.concatenate([turned[j + u] for u in range(GROUP)], axis=1)
            both = jnp.dot(second_ref[...], data, preferred_element_type=jnp.float32)
            for u in range(GROUP):
                part = both[:, u * width : (u + 1) * width]
                window_ref[start + j + u] = part[:S] + turn_lanes(part[S:], sign)
        return carry

    lax.fori_loop(0, W // 8, second, 0)

    def third(i, carry):
        start = pl.multiple_of(i * 8, 8)
        windows = jnp.swapaxes(window_ref[:, pl.ds(start, 8), :], 0, 1)
        out_ref[pl.ds(start, 8), 0] = windows.astype(jnp.bfloat16)
        return carry

    lax.fori_loop(0, S // 8, third, 0)

    @pl.when(pl.program_id(0) == pl.num_programs(0) - 1)
    def _():
        for copy in copies:
            copy.wait_recv()
        for copy in copies:
            copy.wait_send()
        gathered_ref[...] = everyone_ref[...]


def turn_lanes(values, sign):
    return pltpu.roll(values, W, 1) * sign


def transform(strips, coords, device_count):
    vmem = pl.BlockSpec(memory_space=pltpu.VMEM)
    facet_local = strips.shape[0]
    whole = lambda *shape: pl.BlockSpec(shape, lambda f: (0,) * len(shape))
    turns = [
        jnp.broadcast_to(table.T[:, :, None], (S, W, 2 * W)) for table in turn_table(W, S, FH)
    ]
    windows, everyone = pl.pallas_call(
        functools.partial(transform_kernel, device_count),
        out_shape=[
            jax.ShapeDtypeStruct((S, facet_local // 2, W, 4 * W), jnp.bfloat16),
            jax.ShapeDtypeStruct((device_count,) + coords.shape, jnp.float32),
        ],
        grid=(facet_local,),
        in_specs=[
            whole(2 * W, W),
            whole(2 * S, S),
            vmem,
            vmem,
            pl.BlockSpec(memory_space=pl.ANY),
            pl.BlockSpec((1, W, S, 2 * W), lambda f: (f, 0, 0, 0)),
        ],
        out_specs=[pl.BlockSpec((S, 1, W, 2 * W), lambda f: (0, f // 2, 0, f % 2)), vmem],
        scratch_shapes=[
            pltpu.VMEM((S, W, 2 * W), jnp.float32),
            pltpu.VMEM((W, S, 2 * W), jnp.float32),
            pltpu.VMEM((device_count,) + coords.shape, jnp.float32),
            pltpu.SemaphoreType.DMA,
            pltpu.SemaphoreType.DMA((device_count - 1,)),
            pltpu.SemaphoreType.DMA((device_count - 1,)),
        ],
        compiler_params=pltpu.CompilerParams(
            vmem_limit_bytes=28 * 2**20, collective_id=0, has_side_effects=True
        ),
        cost_estimate=pl.CostEstimate(
            flops=5 * 10**10, bytes_accessed=64 * 2**20, transcendentals=0
        ),
    )(
        jnp.concatenate(dft_tables(W), axis=0),
        jnp.concatenate(dft_tables(S), axis=0),
        *turns,
        coords,
        strips.reshape(facet_local, W, S, 2 * W),
    )
    return windows.reshape(S, facet_local // 2 * W, 4 * W), everyone


def predict_kernel(
    facet_local, capacity, index_ref, owners_ref, counts_ref, coords_ref, windows_ref, parts_ref,
    out_ref, items_ref, loads_ref
):
    device_count = out_ref.shape[0]
    max_blocks = out_ref.shape[3]
    uppers = facet_local // 2
    scale = 1.0 / (math.sqrt(FH) * SG)
    row_start = ((index_ref[0] * facet_local) // R * W - SG // 2).astype(jnp.float32)
    col_start = ((index_ref[0] * facet_local) % R * W - SG // 2).astype(jnp.float32)
    out_ref[...] = jnp.zeros_like(out_ref)

    def clear(i, carry):
        loads_ref[i] = 0
        return carry

    lax.fori_loop(0, device_count, clear, 0)

    def list_items(s, total):
        owner = owners_ref[s]
        load = loads_ref[owner]
        loads_ref[owner] = load + 1
        place = (s * device_count + owner) * capacity + load

        def add(b, t):
            items_ref[t] = place * max_blocks + b
            return t + 1

        return lax.fori_loop(0, counts_ref[s], add, total)

    total = lax.fori_loop(0, owners_ref.shape[0], list_items, 0)

    def pad(i, carry):
        items_ref[total + i] = items_ref[total - 1]
        return carry

    lax.fori_loop(0, UNROLL - 1, pad, 0)
    lane = out_ref.shape[4]
    ramp = lax.broadcasted_iota(jnp.int32, (8, lane), 0).astype(jnp.float32)

    def one(item):
        b = item % max_blocks
        place = item // max_blocks
        load = place % capacity
        owner = (place // capacity) % device_count
        s = place // (capacity * device_count)
        x = coords_ref[owner, 0, load, pl.ds(b, 1), :]
        y = coords_ref[owner, 1, load, pl.ds(b, 1), :]
        fine = phase(y, ramp)
        upper = phase(y, jnp.where(ramp < uppers, ramp * (2.0 * W) + col_start, 1.0 * W))
        coarse = phase(y, ramp * 8.0)
        coarse = [coarse, twice(coarse, (upper[0][uppers:uppers + 1], upper[1][uppers:uppers + 1]))]
        cos_rows, sin_rows, neg_rows = [], [], []
        for half in coarse:
            c, s_ = half
            cc, ss = twice(
                (c[:, None, :], s_[:, None, :]), (fine[0][None], fine[1][None])
            )
            cos_rows.append(cc.reshape(W, lane).astype(jnp.bfloat16))
            sin_rows.append(ss.reshape(W, lane).astype(jnp.bfloat16))
            neg_rows.append(-sin_rows[-1])
        table = jnp.concatenate(
            [
                jnp.concatenate([cos_rows[0], sin_rows[0], cos_rows[1], sin_rows[1]], axis=0),
                jnp.concatenate([neg_rows[0], cos_rows[0], neg_rows[1], cos_rows[1]], axis=0),
            ],
            axis=1,
        )
        grid = jnp.dot(windows_ref[s], table, preferred_element_type=jnp.float32)
        row_coarse = phase(x, ramp * 8.0 + row_start)
        row_fine = phase(x, ramp)
        sum_real = jnp.zeros((8, lane), jnp.float32)
        sum_imag = jnp.zeros((8, lane), jnp.float32)
        for h in range(uppers):
            mixed = twice((upper[0][h : h + 1], upper[1][h : h + 1]), row_coarse)
            part = grid[h * W : (h + 1) * W].reshape(8, 8, 2 * lane)
            real, imag = part[:, :, :lane], part[:, :, lane:]
            mc, ms = mixed[0][:, None, :], mixed[1][:, None, :]
            sum_real = sum_real + jnp.sum(real * mc + imag * ms, axis=0)
            sum_imag = sum_imag + jnp.sum(imag * mc - real * ms, axis=0)
        fc, fs = row_fine
        vis_real = jnp.sum(sum_real * fc + sum_imag * fs, axis=0, keepdims=True) * scale
        vis_imag = jnp.sum(sum_imag * fc - sum_real * fs, axis=0, keepdims=True) * scale
        return owner, load, b, vis_real, vis_imag

    def step(i, carry):
        for owner, load, b, vis_real, vis_imag in [
            one(items_ref[i * UNROLL + u]) for u in range(UNROLL)
        ]:
            out_ref[owner, load, 0, pl.ds(b, 1), :] = vis_real
            out_ref[owner, load, 1, pl.ds(b, 1), :] = vis_imag
        return carry

    lax.fori_loop(0, (total + UNROLL - 1) // UNROLL, step, 0)
    parts_ref[...] = out_ref[...].astype(jnp.bfloat16)


def predict(windows, owners, counts, coords, device_index):
    device_count, _, capacity, max_blocks, lane = coords.shape
    facet_local = windows.shape[1] // W * 2
    smem = pl.BlockSpec(memory_space=pltpu.SMEM)
    vmem = pl.BlockSpec(memory_space=pltpu.VMEM)
    slots = (device_count, capacity, 2, max_blocks, lane)
    return pl.pallas_call(
        functools.partial(predict_kernel, facet_local, capacity),
        out_shape=jax.ShapeDtypeStruct(slots, jnp.bfloat16),
        in_specs=[smem, smem, smem, vmem, vmem],
        out_specs=vmem,
        scratch_shapes=[
            pltpu.VMEM(slots, jnp.float32),
            pltpu.SMEM((owners.shape[0] * max_blocks + UNROLL,), jnp.int32),
            pltpu.SMEM((device_count,), jnp.int32),
        ],
        compiler_params=pltpu.CompilerParams(vmem_limit_bytes=16 * 2**20),
    )(device_index.reshape(1), owners, counts, coords, windows)


def add_up_kernel(
    device_count, pols, in_ref, out_ref, arrived_ref, total_ref, send_sem, recv_sem, pol_send_sem,
    pol_recv_sem
):
    me = lax.axis_index("fs")
    pol = lax.axis_index("pol")
    peers = [{"fs": lax.rem(me + step, device_count)} for step in range(1, device_count)]
    pol_peers = [{"pol": lax.rem(pol + step, pols)} for step in range(1, pols)]
    barrier = pltpu.get_barrier_semaphore()
    for peer in peers + pol_peers:
        pl.semaphore_signal(
            barrier, inc=1, device_id=peer, device_id_type=pl.DeviceIdType.MESH
        )
    pl.semaphore_wait(barrier, device_count + pols - 2)
    copies = []
    for i, peer in enumerate(peers):
        copy = pltpu.make_async_remote_copy(
            src_ref=in_ref.at[peer["fs"]],
            dst_ref=arrived_ref.at[i],
            send_sem=send_sem.at[i],
            recv_sem=recv_sem.at[i],
            device_id=peer,
            device_id_type=pl.DeviceIdType.MESH,
        )
        copy.start()
        copies.append(copy)
    total_ref[pol] = in_ref[me].astype(jnp.float32)
    for i, copy in enumerate(copies):
        copy.wait_recv()
        total_ref[pol] += arrived_ref[i].astype(jnp.float32)
    pol_copies = []
    for i, peer in enumerate(pol_peers):
        copy = pltpu.make_async_remote_copy(
            src_ref=total_ref.at[pol],
            dst_ref=total_ref.at[pol],
            send_sem=pol_send_sem.at[i],
            recv_sem=pol_recv_sem.at[i],
            device_id=peer,
            device_id_type=pl.DeviceIdType.MESH,
        )
        copy.start()
        pol_copies.append(copy)
    for copy in pol_copies:
        copy.wait_recv()
    for copy in copies + pol_copies:
        copy.wait_send()
    out_ref[...] = total_ref[...]


def add_up(parts, pols):
    device_count = parts.shape[0]
    vmem = pl.BlockSpec(memory_space=pltpu.VMEM)
    return pl.pallas_call(
        functools.partial(add_up_kernel, device_count, pols),
        out_shape=jax.ShapeDtypeStruct((pols,) + parts.shape[1:], jnp.float32),
        in_specs=[vmem],
        out_specs=vmem,
        scratch_shapes=[
            pltpu.VMEM((device_count - 1,) + parts.shape[1:], jnp.bfloat16),
            pltpu.VMEM((pols,) + parts.shape[1:], jnp.float32),
            pltpu.SemaphoreType.DMA((device_count - 1,)),
            pltpu.SemaphoreType.DMA((device_count - 1,)),
            pltpu.SemaphoreType.DMA((pols - 1,)),
            pltpu.SemaphoreType.DMA((pols - 1,)),
        ],
        compiler_params=pltpu.CompilerParams(collective_id=1, has_side_effects=True),
    )(parts)


def correct_kernel(index_ref, owners_ref, counts_ref, left_ref, right_ref, table_ref, vis_ref, out_ref):
    capacity = out_ref.shape[1]
    max_blocks, lane = out_ref.shape[2:]
    chunks = table_ref.shape[1] // lane
    me = index_ref[0]
    out_ref[...] = jnp.zeros_like(out_ref)
    block = lax.broadcasted_iota(jnp.int32, (max_blocks, lane), 0)

    def look_up(first, ids):
        low = ids % lane
        high = ids // lane
        found = []
        for row in range(4):
            entry = None
            for chunk in range(chunks):
                source = jnp.broadcast_to(
                    table_ref[first + row : first + row + 1, chunk * lane : (chunk + 1) * lane],
                    (max_blocks, lane),
                )
                got = jnp.take_along_axis(source, low, axis=1, mode="promise_in_bounds")
                entry = got if entry is None else jnp.where(high == chunk, got, entry)
            found.append(entry)
        return [(found[0], found[1]), (found[2], found[3])]

    def product(a, b):
        return (a[0] * b[0] - a[1] * b[1], a[0] * b[1] + a[1] * b[0])

    def slot(s, load):
        is_mine = owners_ref[s] == me

        @pl.when(is_mine)
        def _():
            left = look_up(0, left_ref[load])
            right = look_up(4, right_ref[load])
            total_real = jnp.zeros((max_blocks, lane), jnp.float32)
            total_imag = jnp.zeros((max_blocks, lane), jnp.float32)
            for inner_row in range(2):
                for inner_col in range(2):
                    comp = 2 * inner_row + inner_col
                    step = product(
                        left[inner_row], (vis_ref[comp, load, 0], vis_ref[comp, load, 1])
                    )
                    step = product(step, (right[inner_col][0], -right[inner_col][1]))
                    total_real = total_real + step[0]
                    total_imag = total_imag + step[1]
            keep = block < counts_ref[s]
            out_ref[0, load] = jnp.where(keep, total_real, 0.0)
            out_ref[1, load] = jnp.where(keep, total_imag, 0.0)

        return load + is_mine.astype(jnp.int32)

    lax.fori_loop(0, owners_ref.shape[0], slot, 0)


def correct(visible, owners, counts, station_ids, tables, device_index):
    _, capacity, _, max_blocks, lane = visible.shape
    smem = pl.BlockSpec(memory_space=pltpu.SMEM)
    vmem = pl.BlockSpec(memory_space=pltpu.VMEM)
    return pl.pallas_call(
        correct_kernel,
        out_shape=jax.ShapeDtypeStruct((2, capacity, max_blocks, lane), jnp.float32),
        in_specs=[smem, smem, smem, vmem, vmem, vmem, vmem],
        out_specs=vmem,
    )(
        device_index.reshape(1),
        owners,
        counts,
        station_ids[:, :, 0, :],
        station_ids[:, :, 1, :],
        tables,
        visible,
    )


def on_device(facets, owners, counts, coords, station_ids, jones_table):
    device_index = lax.axis_index("fs").astype(jnp.int32)
    pol_index = lax.axis_index("pol")
    device_count, pols = lax.axis_size("fs"), lax.axis_size("pol")
    windows, all_coords = transform(facets[0], coords, device_count)
    visible = add_up(predict(windows, owners, counts, all_coords, device_index), pols)
    tables = jnp.concatenate(
        [
            lax.dynamic_slice_in_dim(jones_table, 4 * (pol_index // 2), 4, 0),
            lax.dynamic_slice_in_dim(jones_table, 4 * (pol_index % 2), 4, 0),
        ],
        axis=0,
    )
    return correct(visible, owners, counts, station_ids, tables, device_index)[None]


def solution(mesh):
    return jax.shard_map(
        on_device,
        mesh=mesh,
        in_specs=(
            P("pol", "fs", None, None),
            P(),
            P(),
            P(None, "fs", None, None),
            P("fs", None, None, None),
            P(),
        ),
        out_specs=P("pol", None, "fs", None, None),
        check_vma=False,
    )
```

profile of v0, /device:TPU:11, one launch (start us, length us, event | category | flops | bytes accessed | tf_op | source)
XLA Modules:
  0.0 130.3 jit_solution(16878532592814315712)
XLA Ops:
  0.0 0.8 constant_dynamic-slice_fusion.1
  0.8 0.6 pad_maximum_fusion.1.table_ref
  1.4 0.2 sine_convert_fusion
  1.6 0.1 fusion.12
  1.7 0.6 broadcast_in_dim.6.turn_cos_ref
  2.3 0.1 fusion.11
  2.5 0.6 broadcast_in_dim.7.turn_sin_ref
  3.1 0.0 copy-start.5
  3.1 3.4 %copy-done.5 = bf16[1,8,4096,128]{3,2,1,0:T(8,128)(2,1)S(1)} copy-done((bf16[1,8,4096,128]{3,2,1,0:T(8,128)(2,1)S(1)}, bf16[1,8,4096,128]{3,2,1,0:T(8,128)(2,1)}, u32[]{:S(2)}) %copy-start.5) | copy-done | bytes 8388632
  6.5 0.0 copy-start.6
  6.5 0.9 copy-done.6
  7.4 0.0 copy-start.3
  7.4 0.0 copy-start.4
  7.4 0.0 copy-start.7
  7.4 44.7 %shard_map.64 = (bf16[64,4,64,256]{3,2,1,0:T(8,128)(2,1)S(1)}, f32[8,2,16,8,128]{4,3,2,1,0:T(8,128)S(1)}) custom-call(bf16[128,64]{1,0:T(8,128)(2,1)S(1)} %pad_maximum_fusion.first_ref.second_ref, bf16[128,64]{1,0:T(8,128)(2,1)S(1)} %pad_maximum_fusion.first_ref.second_ref, f32[64,64,128]{2,1,0:T(8,128)S(1)} %broadcast_in_dim.6.turn_cos_ref, ...), custom_call_target="tpu_custom_call" | custom-call | flops 49999998976 | bytes 67108864 | tf_op jit(solution)/shard_map/pallas_call | solution.py:162
  52.1 0.0 copy-start
  52.1 3.2 %copy-done = bf16[64,4,64,256]{3,2,1,0:T(8,128)(2,1)} copy-done((bf16[64,4,64,256]{3,2,1,0:T(8,128)(2,1)}, bf16[64,4,64,256]{3,2,1,0:T(8,128)(2,1)S(1)}, u32[]{:S(2)}) %copy-start) | copy-done | bytes 8388632
  55.3 0.0 copy-done.3
  55.3 0.0 copy-done.4
  55.3 0.0 copy-start.1
  55.3 3.4 %copy-done.1 = bf16[64,4,64,256]{3,2,1,0:T(8,128)(2,1)S(1)} copy-done((bf16[64,4,64,256]{3,2,1,0:T(8,128)(2,1)S(1)}, bf16[64,4,64,256]{3,2,1,0:T(8,128)(2,1)}, u32[]{:S(2)}) %copy-start.1) | copy-done | bytes 8388632
  58.7 41.1 %shard_map.65.in_ref = bf16[8,16,2,8,128]{4,3,2,1,0:T(8,128)(2,1)S(1)} custom-call(s32[1]{0:T(128)} %bitcast.index_ref, s32[64]{0:T(128)S(1)} %copy-done.3, s32[64]{0:T(128)S(1)} %copy-done.4, f32[8,2,16,8,128]{4,3,2,1,0:T(8,128)S(1)} %get-tuple-element.7.coords_ref, bf16[64,256,256]{2,1,0:T(8,128)(2,1)S(1)} %bitcast.10), custom_call_target="tpu_custom_call" | custom-call | tf_op jit(solution)/shard_map/pallas_call | solution.py:305
  99.8 0.0 copy-start.2
  99.9 0.8 copy-done.2
  100.6 24.4 %shard_map.66.vis_ref = f32[4,16,2,8,128]{4,3,2,1,0:T(8,128)} custom-call(bf16[8,16,2,8,128]{4,3,2,1,0:T(8,128)(2,1)} %copy-done.2), custom_call_target="tpu_custom_call" | custom-call | tf_op jit(solution)/shard_map/pallas_call | solution.py:371
  125.0 0.0 copy-done.7
  125.0 0.7 fusion.13
  125.7 4.6 %shard_map.67 = f32[2,16,8,128]{3,2,1,0:T(8,128)} custom-call(s32[1]{0:T(128)} %bitcast.index_ref, s32[64]{0:T(128)} %owners_ref.3, s32[64]{0:T(128)} %counts_ref.3, s32[16,8,128]{2,1,0:T(8,128)} %bitcast.13, s32[16,8,128]{2,1,0:T(8,128)} %bitcast.12, f32[8,512]{1,0:T(8,128)} %pad_maximum_fusion.1.table_ref, f32[4,16,2,8,128]{4,3,2,1,0:T(8,128)} %shard_map.66.vis_ref), custom_call_target="tpu_custom_call" | custom-call | tf_op jit(solution)/shard_map/pallas_call | solution.py:446
  (1 shorter events, 0.0 us)
Async XLA Ops:
  3.1 3.4 %copy-start.5 = (bf16[1,8,4096,128]{3,2,1,0:T(8,128)(2,1)S(1)}, bf16[1,8,4096,128]{3,2,1,0:T(8,128)(2,1)}, u32[]{:S(2)}) copy-start(bf16[1,8,4096,128]{3,2,1,0:T(8,128)(2,1)} %param.6) | copy-start | bytes 25165828
  6.5 0.9 copy-start.6
  7.4 47.9 %copy-start.3 = (s32[64]{0:T(128)S(1)}, s32[64]{0:T(128)}, u32[]{:S(2)}) copy-start(s32[64]{0:T(128)} %owners_ref.3) | copy-start | bytes 772
  7.4 47.9 %copy-start.4 = (s32[64]{0:T(128)S(1)}, s32[64]{0:T(128)}, u32[]{:S(2)}) copy-start(s32[64]{0:T(128)} %counts_ref.3) | copy-start | bytes 772
  7.4 117.6 %copy-start.7 = (s32[16,8,2,128]{3,2,1,0:T(2,128)S(1)}, s32[16,8,2,128]{3,2,1,0:T(2,128)}, u32[]{:S(2)}) copy-start(s32[16,8,2,128]{3,2,1,0:T(2,128)} %param.10) | copy-start | bytes 393220
  52.1 3.2 %copy-start = (bf16[64,4,64,256]{3,2,1,0:T(8,128)(2,1)}, bf16[64,4,64,256]{3,2,1,0:T(8,128)(2,1)S(1)}, u32[]{:S(2)}) copy-start(bf16[64,4,64,256]{3,2,1,0:T(8,128)(2,1)S(1)} %get-tuple-element.8) | copy-start | bytes 25165828
  55.3 3.4 %copy-start.1 = (bf16[64,4,64,256]{3,2,1,0:T(8,128)(2,1)S(1)}, bf16[64,4,64,256]{3,2,1,0:T(8,128)(2,1)}, u32[]{:S(2)}) copy-start(bf16[64,4,64,256]{3,2,1,0:T(8,128)(2,1)} %copy-done) | copy-start | bytes 25165828
  99.8 0.8 copy-start.2
where the time goes:
time: 131 us; the launch traced here: 130 us
  Pallas kernels  115 us (88%)
  local copies, waits for them, and re-layouts  14.4 us (11%)
    pallas_call x1, Pallas kernels, transform(): pl.pallas_call(functools.partial(transform_kernel, device_count), out_sha...  44.7 us
    pallas_call x1, Pallas kernels, predict(): pl.pallas_call(functools.partial(predict_kernel, facet_local, capacity),...  41.1 us
    pallas_call x1, Pallas kernels, add_up(): pl.pallas_call(functools.partial(add_up_kernel, device_count, pols), out_...  24.4 us
    unnamed x16, local copies, waits for them, and re-layouts  11.7 us
    pallas_call x1, Pallas kernels, correct(): pl.pallas_call(correct_kernel, out_shape=jax.ShapeDtypeStruct((2, capacit...  4.55 us

commit v1 on v0

v1 whole, which is shorter than its diff:
```python
import functools
import math

import jax
import jax.numpy as jnp
import numpy as np
from jax import lax
from jax.experimental import pallas as pl
from jax.experimental.pallas import tpu as pltpu
from jax.sharding import PartitionSpec as P

R = 8
W = 64
S = 64
FH = 4096
SG = 512
LANES = 128
SPAN = 4
PITCH = 65
CHUNK = 1024
UNROLL = 8
PAIRS = 4


def fit(values, terms):
    series = np.polynomial.chebyshev.Chebyshev.interpolate(
        lambda square: values(np.sqrt(np.maximum(square, 1e-12))), terms - 1, domain=[0.0, 0.25]
    )
    return [float(c) for c in series.convert(kind=np.polynomial.Polynomial).coef]


SIN_COEFS = fit(lambda r: np.sin(np.pi * r) / r, 5)
COS_COEFS = fit(lambda r: np.cos(np.pi * r), 5)


def unit_circle(turns):
    return np.exp(-2j * np.pi * turns)


def as_real(table):
    return np.concatenate(
        [
            np.concatenate([table.real, -table.imag], axis=-1),
            np.concatenate([table.imag, table.real], axis=-1),
        ],
        axis=-2,
    )


def mix_table():
    table = np.zeros((4 * W, 4 * W))
    col = np.arange(W)
    mirror = W - 1 - col
    a_real, a_imag, b_real, b_imag = mirror, W + mirror, 2 * W + col, 3 * W + col
    table[b_real, col] = table[a_real, col] = 1.0
    table[b_imag, W + col] = 1.0
    table[a_imag, W + col] = -1.0
    table[b_imag, 2 * W + col] = table[a_imag, 2 * W + col] = 1.0
    table[b_real, 3 * W + col] = -1.0
    table[a_real, 3 * W + col] = 1.0
    return table


def first_tables():
    n1 = np.arange(S)[:, None, None]
    k1 = np.arange(W)[None, :, None]
    n2 = np.arange(W)[None, None, :]
    rows = unit_circle((k1 * n2 % W) / W + (n1 * k1 % FH) / FH)
    upper, lower = rows[:, W // 2 :], rows[:, W // 2 - 1 :: -1]
    return as_real(np.concatenate([upper + lower, -1j * (upper - lower)], axis=1))


def second_table():
    index = np.arange(S)
    table = unit_circle((index[:, None] * index[None, :] % S) / S)
    return as_real(table) / (math.sqrt(FH) * SG)


def horner(coefs, square):
    total = jnp.full_like(square, coefs[-1])
    for coef in coefs[-2::-1]:
        total = total * square + coef
    return total


def phase(turns):
    rest = turns - jnp.round(turns)
    square = rest * rest
    half_cos = horner(COS_COEFS, square)
    half_sin = horner(SIN_COEFS, square) * rest
    double = half_sin + half_sin
    return 1.0 - double * half_sin, double * half_cos


def twice(left, right):
    return (left[0] * right[0] - left[1] * right[1], left[1] * right[0] + left[0] * right[1])


def chain(start, step, count):
    terms = [start, twice(start, step)]
    double = step[0] + step[0]
    while len(terms) < count:
        (last_cos, last_sin), (cos, sin) = terms[-2:]
        terms.append((double * cos - last_cos, double * sin - last_sin))
    return terms


def transform_kernel(
    device_count, strips_ref, first_hbm, coords_ref, mix_ref, second_ref, out_ref, gathered_ref,
    strip_ref, first_ref, mixed_ref, turned_ref, everyone_ref, strip_sem, first_sem, own_sem,
    send_sem, recv_sem, pair_send_sem, pair_recv_sem
):
    me = lax.axis_index("fs")
    pol = lax.axis_index("pol")
    half = lax.rem(pol, 2)
    partner = {"pol": pol + 1 - 2 * half}
    facet_local = strip_ref.shape[0]
    slots = everyone_ref.shape[2] // 2
    span = min(SPAN, facet_local)
    pairs = span // 2

    order = []
    for group in range(facet_local // span):
        for pair in range(pairs):
            low = group * span + pairs - 1 - pair
            order.append((low, low + 2 * pair + 1))
    loads = [
        pltpu.make_async_copy(strips_ref.at[f], strip_ref.at[f], strip_sem.at[f])
        for f in range(facet_local)
    ]
    for low, high in order:
        loads[low].start()
        loads[high].start()
    tables = pltpu.make_async_copy(first_hbm, first_ref, first_sem)
    tables.start()
    own = pltpu.make_async_copy(coords_ref, everyone_ref.at[me], own_sem)
    own.start()

    barrier = pltpu.get_barrier_semaphore()
    for step in range(1, device_count):
        pl.semaphore_signal(
            barrier,
            inc=1,
            device_id={"fs": lax.rem(me + step, device_count)},
            device_id_type=pl.DeviceIdType.MESH,
        )
    pl.semaphore_signal(barrier, inc=1, device_id=partner, device_id_type=pl.DeviceIdType.MESH)
    pl.semaphore_wait(barrier, device_count)
    own.wait()
    sends = []
    for step in range(1, device_count):
        mine = everyone_ref.at[me, :, pl.ds(half * slots, slots)]
        copy = pltpu.make_async_remote_copy(
            src_ref=mine,
            dst_ref=mine,
            send_sem=send_sem.at[step - 1],
            recv_sem=recv_sem.at[step - 1],
            device_id={"fs": lax.rem(me + step, device_count)},
            device_id_type=pl.DeviceIdType.MESH,
        )
        copy.start()
        sends.append(copy)

    def lanes(pieces):
        return jnp.concatenate(pieces, axis=1).astype(jnp.bfloat16)

    for group in range(facet_local // span):
        for pair in range(pairs):
            low, high = order[group * pairs + pair]
            loads[low].wait()
            loads[high].wait()

            def mix(i, carry, low=low, high=high, pair=pair):
                rows = pl.ds(pl.multiple_of(i * CHUNK, CHUNK), CHUNK)
                both = jnp.dot(
                    jnp.concatenate([strip_ref[low, rows, :], strip_ref[high, rows, :]], axis=1),
                    mix_ref[...],
                    preferred_element_type=jnp.float32,
                )
                for t in range(CHUNK // W):
                    to = pl.ds((i * (CHUNK // W) + t) * PITCH, W)
                    for part in range(2):
                        mixed_ref[2 * pair + part, to, :] = both[
                            W * t : W * (t + 1), LANES * part : LANES * (part + 1)
                        ]
                return carry

            lax.fori_loop(0, FH // CHUNK, mix, 0)
        if group == 0:
            tables.wait()

        def put(to_ref, rows, product):
            for pair in range(pairs):
                for part in range(2):
                    to_ref[2 * pair + part, rows, :] = product[
                        W * part : W * (part + 1), LANES * pair : LANES * (pair + 1)
                    ]

        def take(from_ref, rows):
            return jnp.concatenate(
                [lanes([from_ref[2 * q + part, rows, :] for q in range(pairs)]) for part in range(2)],
                axis=0,
            )

        def first(i, carry):
            for u in range(UNROLL):
                rows = pl.ds(i * UNROLL + u, W, stride=PITCH)
                put(
                    turned_ref,
                    rows,
                    jnp.dot(
                        first_ref[i * UNROLL + u],
                        take(mixed_ref, rows),
                        preferred_element_type=jnp.float32,
                    ),
                )
            return carry

        lax.fori_loop(0, S // UNROLL, first, 0)

        def second(i, carry):
            for u in range(UNROLL):
                k = i * UNROLL + u
                put(
                    mixed_ref,
                    pl.ds(k, S, stride=PITCH),
                    jnp.dot(
                        second_ref[...],
                        take(turned_ref, pl.ds(k * PITCH, S)),
                        preferred_element_type=jnp.float32,
                    ),
                )
            return carry

        lax.fori_loop(0, W // UNROLL, second, 0)

        def third(i, carry, group=group):
            for u in range(2):
                s = i * 2 + u
                out_ref[s, pl.ds(group * 2 * W, 2 * W), :] = take(mixed_ref, pl.ds(s * PITCH, W))
            return carry

        lax.fori_loop(0, S // 2, third, 0)

    forwards = []
    for step in range(1, device_count):
        sends[step - 1].wait_recv()
        theirs = everyone_ref.at[
            lax.rem(me + device_count - step, device_count), :, pl.ds(half * slots, slots)
        ]
        copy = pltpu.make_async_remote_copy(
            src_ref=theirs,
            dst_ref=theirs,
            send_sem=pair_send_sem.at[step - 1],
            recv_sem=pair_recv_sem.at[step - 1],
            device_id=partner,
            device_id_type=pl.DeviceIdType.MESH,
        )
        copy.start()
        forwards.append(copy)
    for copy in forwards:
        copy.wait_recv()
    for copy in sends + forwards:
        copy.wait_send()
    gathered_ref[...] = everyone_ref[...]


def transform(strips, coords, device_count):
    vmem = pl.BlockSpec(memory_space=pltpu.VMEM)
    anywhere = pl.BlockSpec(memory_space=pl.ANY)
    facet_local = strips.shape[0]
    span = min(SPAN, facet_local)
    scratch = pltpu.VMEM((span, S * PITCH, LANES), jnp.float32)
    constant = lambda table: jnp.asarray(table, jnp.bfloat16)
    return pl.pallas_call(
        functools.partial(transform_kernel, device_count),
        out_shape=[
            jax.ShapeDtypeStruct((S, facet_local // span * 2 * W, span * W), jnp.bfloat16),
            jax.ShapeDtypeStruct((device_count,) + coords.shape, jnp.float32),
        ],
        in_specs=[anywhere, anywhere, anywhere, vmem, vmem],
        out_specs=[vmem, vmem],
        scratch_shapes=[
            pltpu.VMEM((facet_local, FH, LANES), jnp.bfloat16),
            pltpu.VMEM((S, 2 * W, 2 * W), jnp.bfloat16),
            scratch,
            scratch,
            pltpu.VMEM((device_count,) + coords.shape, jnp.float32),
            pltpu.SemaphoreType.DMA((facet_local,)),
            pltpu.SemaphoreType.DMA,
            pltpu.SemaphoreType.DMA,
            pltpu.SemaphoreType.DMA((device_count - 1,)),
            pltpu.SemaphoreType.DMA((device_count - 1,)),
            pltpu.SemaphoreType.DMA((device_count - 1,)),
            pltpu.SemaphoreType.DMA((device_count - 1,)),
        ],
        compiler_params=pltpu.CompilerParams(
            vmem_limit_bytes=42 * 2**20, collective_id=0, has_side_effects=True
        ),
        cost_estimate=pl.CostEstimate(
            flops=5 * 10**9, bytes_accessed=16 * 2**20, transcendentals=0
        ),
    )(strips, constant(first_tables()), coords, constant(mix_table()), constant(second_table()))


def predict_kernel(
    facet_local, index_ref, owners_ref, counts_ref, coords_ref, windows_ref, parts_ref, out_ref,
    table_ref, row_ref, place_ref, loads_ref
):
    device_count = out_ref.shape[0]
    lane = out_ref.shape[4]
    subgrids = owners_ref.shape[0]
    span = min(SPAN, facet_local)
    groups = facet_local // span
    steps = span // 2
    first = index_ref[0] * facet_local
    unit = 1.0 / SG
    row_middle = (lax.div(first, R) * W).astype(jnp.float32) + (0.5 * (W - 1) - SG // 2)
    col_middle = (lax.rem(first, R) * W).astype(jnp.float32) + (0.5 * (span * W - 1) - SG // 2)
    ramp = lax.broadcasted_iota(jnp.int32, (8, lane), 0).astype(jnp.float32)
    fine = (ramp + 0.5) * unit
    col_pick = jnp.where(ramp == 1.0, 0.0, col_middle + (ramp - 2.0) * (span * W))
    col_pick = jnp.where(ramp == 0.0, 8.0, col_pick) * unit
    row_pick = jnp.where(ramp == 0.0, 0.0, jnp.where(ramp == 1.0, 8.0, row_middle)) * unit
    out_ref[...] = jnp.zeros_like(out_ref)

    def clear(i, carry):
        loads_ref[i] = 0
        return carry

    lax.fori_loop(0, device_count, clear, 0)

    def rank(s, total):
        owner = owners_ref[s]
        load = loads_ref[owner]
        loads_ref[owner] = load + 1
        place_ref[s] = load
        return total + lax.div(counts_ref[s] + 1, 2)

    total = lax.fori_loop(0, subgrids, rank, 0)

    def following(s, b):
        items = []
        for _ in range(PAIRS):
            items.append((s, b))
            done = b + 2 >= counts_ref[s]
            end = jnp.logical_and(done, s == subgrids - 1)
            b = jnp.where(end, b, jnp.where(done, 0, b + 2))
            s = jnp.where(done, jnp.minimum(s + 1, subgrids - 1), s)
        return items, (s, b)

    def tables(u, turn, s, b):
        owner, load = owners_ref[s], place_ref[s]
        for h in range(2):
            x = coords_ref[owner, 0, load, pl.ds(b + h, 1), :]
            y = coords_ref[owner, 1, load, pl.ds(b + h, 1), :]
            picked = phase(x * row_pick + y * col_pick)
            col_step, row_step = [
                [jnp.broadcast_to(part[i : i + 1], (8, lane)) for part in picked] for i in range(2)
            ]
            cols = chain(phase(y * fine), col_step, steps * W // 8)
            entries = []
            for k in range(steps):
                some = cols[W // 8 * k : W // 8 * (k + 1)]
                entries += [cos for cos, _ in some] + [sin for _, sin in some]
            table_ref[u, :, h * lane : (h + 1) * lane] = jnp.concatenate(entries, axis=0).astype(
                jnp.bfloat16
            )
            rows = chain(phase(x * fine), row_step, W // 16)
            row_ref[turn, u, h] = jnp.concatenate(
                [cos for cos, _ in rows] + [sin for _, sin in rows] + list(picked), axis=0
            )

    def predict(u, turn, s, b):
        grid = jnp.dot(windows_ref[s], table_ref[u], preferred_element_type=jnp.float32)
        owner, load = owners_ref[s], place_ref[s]
        for h in range(2):
            real = imag = None
            for g in range(groups):
                sums = []
                for part in range(2):
                    total = None
                    for k in range(W // 8):
                        at = (2 * g + part) * W + 8 * k
                        term = grid[at : at + 8, h * lane : (h + 1) * lane] * row_ref[
                            turn, u, h, 8 * k : 8 * k + 8, :
                        ]
                        total = term if total is None else total + term
                    sums.append(total)
                cos = row_ref[turn, u, h, W + 2 + g : W + 3 + g, :]
                sin = row_ref[turn, u, h, W + 10 + g : W + 11 + g, :]
                more_real = sums[0] * cos + sums[1] * sin
                more_imag = sums[1] * cos - sums[0] * sin
                real = more_real if real is None else real + more_real
                imag = more_imag if imag is None else imag + more_imag
            out_ref[owner, load, 0, pl.ds(b + h, 1), :] = jnp.sum(real, axis=0, keepdims=True)
            out_ref[owner, load, 1, pl.ds(b + h, 1), :] = jnp.sum(imag, axis=0, keepdims=True)

    items, after = following(0, 0)
    for u, (s, b) in enumerate(items):
        tables(u, 0, s, b)

    def step(i, carry):
        items, after = carry
        for u, (s, b) in enumerate(items):
            predict(u, i & 1, s, b)
        items, after = following(*after)
        for u, (s, b) in enumerate(items):
            tables(u, (i + 1) & 1, s, b)
        return items, after

    lax.fori_loop(0, lax.div(total + PAIRS - 1, PAIRS), step, (items, after))
    parts_ref[...] = out_ref[...].astype(jnp.bfloat16)


def predict(windows, owners, counts, coords, device_index, facet_local):
    device_count, _, capacity, max_blocks, lane = coords.shape
    smem = pl.BlockSpec(memory_space=pltpu.SMEM)
    vmem = pl.BlockSpec(memory_space=pltpu.VMEM)
    slots = (device_count, capacity, 2, max_blocks, lane)
    return pl.pallas_call(
        functools.partial(predict_kernel, facet_local),
        out_shape=jax.ShapeDtypeStruct(slots, jnp.bfloat16),
        in_specs=[smem, smem, smem, vmem, vmem],
        out_specs=vmem,
        scratch_shapes=[
            pltpu.VMEM(slots, jnp.float32),
            pltpu.VMEM((PAIRS, windows.shape[2], 2 * lane), jnp.bfloat16),
            pltpu.VMEM((2, PAIRS, 2, W + 16, lane), jnp.float32),
            pltpu.SMEM((owners.shape[0],), jnp.int32),
            pltpu.SMEM((device_count,), jnp.int32),
        ],
        compiler_params=pltpu.CompilerParams(vmem_limit_bytes=16 * 2**20),
    )(device_index.reshape(1), owners, counts, coords, windows)


def add_up_kernel(
    device_count, pols, in_ref, out_ref, arrived_ref, total_ref, send_sem, recv_sem, pol_send_sem,
    pol_recv_sem
):
    me = lax.axis_index("fs")
    pol = lax.axis_index("pol")
    peers = [{"fs": lax.rem(me + step, device_count)} for step in range(1, device_count)]
    pol_peers = [{"pol": lax.rem(pol + step, pols)} for step in range(1, pols)]
    barrier = pltpu.get_barrier_semaphore()
    for peer in peers + pol_peers:
        pl.semaphore_signal(
            barrier, inc=1, device_id=peer, device_id_type=pl.DeviceIdType.MESH
        )
    pl.semaphore_wait(barrier, device_count + pols - 2)
    copies = []
    for i, peer in enumerate(peers):
        copy = pltpu.make_async_remote_copy(
            src_ref=in_ref.at[peer["fs"]],
            dst_ref=arrived_ref.at[i],
            send_sem=send_sem.at[i],
            recv_sem=recv_sem.at[i],
            device_id=peer,
            device_id_type=pl.DeviceIdType.MESH,
        )
        copy.start()
        copies.append(copy)
    total_ref[pol] = in_ref[me].astype(jnp.float32)
    for i, copy in enumerate(copies):
        copy.wait_recv()
        total_ref[pol] += arrived_ref[i].astype(jnp.float32)
    pol_copies = []
    for i, peer in enumerate(pol_peers):
        copy = pltpu.make_async_remote_copy(
            src_ref=total_ref.at[pol],
            dst_ref=total_ref.at[pol],
            send_sem=pol_send_sem.at[i],
            recv_sem=pol_recv_sem.at[i],
            device_id=peer,
            device_id_type=pl.DeviceIdType.MESH,
        )
        copy.start()
        pol_copies.append(copy)
    for copy in pol_copies:
        copy.wait_recv()
    for copy in copies + pol_copies:
        copy.wait_send()
    out_ref[...] = total_ref[...]


def add_up(parts, pols):
    device_count = parts.shape[0]
    vmem = pl.BlockSpec(memory_space=pltpu.VMEM)
    return pl.pallas_call(
        functools.partial(add_up_kernel, device_count, pols),
        out_shape=jax.ShapeDtypeStruct((pols,) + parts.shape[1:], jnp.float32),
        in_specs=[vmem],
        out_specs=vmem,
        scratch_shapes=[
            pltpu.VMEM((device_count - 1,) + parts.shape[1:], jnp.bfloat16),
            pltpu.VMEM((pols,) + parts.shape[1:], jnp.float32),
            pltpu.SemaphoreType.DMA((device_count - 1,)),
            pltpu.SemaphoreType.DMA((device_count - 1,)),
            pltpu.SemaphoreType.DMA((pols - 1,)),
            pltpu.SemaphoreType.DMA((pols - 1,)),
        ],
        compiler_params=pltpu.CompilerParams(collective_id=1, has_side_effects=True),
    )(parts)


def correct_kernel(index_ref, owners_ref, counts_ref, left_ref, right_ref, table_ref, vis_ref, out_ref):
    capacity = out_ref.shape[1]
    max_blocks, lane = out_ref.shape[2:]
    chunks = table_ref.shape[1] // lane
    me = index_ref[0]
    out_ref[...] = jnp.zeros_like(out_ref)
    block = lax.broadcasted_iota(jnp.int32, (max_blocks, lane), 0)

    def look_up(first, ids):
        low = ids % lane
        high = ids // lane
        found = []
        for row in range(4):
            entry = None
            for chunk in range(chunks):
                source = jnp.broadcast_to(
                    table_ref[first + row : first + row + 1, chunk * lane : (chunk + 1) * lane],
                    (max_blocks, lane),
                )
                got = jnp.take_along_axis(source, low, axis=1, mode="promise_in_bounds")
                entry = got if entry is None else jnp.where(high == chunk, got, entry)
            found.append(entry)
        return [(found[0], found[1]), (found[2], found[3])]

    def product(a, b):
        return (a[0] * b[0] - a[1] * b[1], a[0] * b[1] + a[1] * b[0])

    def slot(s, load):
        is_mine = owners_ref[s] == me

        @pl.when(is_mine)
        def _():
            left = look_up(0, left_ref[load])
            right = look_up(4, right_ref[load])
            total_real = jnp.zeros((max_blocks, lane), jnp.float32)
            total_imag = jnp.zeros((max_blocks, lane), jnp.float32)
            for inner_row in range(2):
                for inner_col in range(2):
                    comp = 2 * inner_row + inner_col
                    step = product(
                        left[inner_row], (vis_ref[comp, load, 0], vis_ref[comp, load, 1])
                    )
                    step = product(step, (right[inner_col][0], -right[inner_col][1]))
                    total_real = total_real + step[0]
                    total_imag = total_imag + step[1]
            keep = block < counts_ref[s]
            out_ref[0, load] = jnp.where(keep, total_real, 0.0)
            out_ref[1, load] = jnp.where(keep, total_imag, 0.0)

        return load + is_mine.astype(jnp.int32)

    lax.fori_loop(0, owners_ref.shape[0], slot, 0)


def correct(visible, owners, counts, station_ids, tables, device_index):
    _, capacity, _, max_blocks, lane = visible.shape
    smem = pl.BlockSpec(memory_space=pltpu.SMEM)
    vmem = pl.BlockSpec(memory_space=pltpu.VMEM)
    return pl.pallas_call(
        correct_kernel,
        out_shape=jax.ShapeDtypeStruct((2, capacity, max_blocks, lane), jnp.float32),
        in_specs=[smem, smem, smem, vmem, vmem, vmem, vmem],
        out_specs=vmem,
    )(
        device_index.reshape(1),
        owners,
        counts,
        station_ids[:, :, 0, :],
        station_ids[:, :, 1, :],
        tables,
        visible,
    )


def on_device(facets, owners, counts, coords, station_ids, jones_table):
    device_index = lax.axis_index("fs").astype(jnp.int32)
    pol_index = lax.axis_index("pol")
    device_count, pols = lax.axis_size("fs"), lax.axis_size("pol")
    windows, all_coords = transform(facets[0], coords, device_count)
    parts = predict(windows, owners, counts, all_coords, device_index, facets.shape[1])
    visible = add_up(parts, pols)
    tables = jnp.concatenate(
        [
            lax.dynamic_slice_in_dim(jones_table, 4 * (pol_index // 2), 4, 0),
            lax.dynamic_slice_in_dim(jones_table, 4 * (pol_index % 2), 4, 0),
        ],
        axis=0,
    )
    return correct(visible, owners, counts, station_ids, tables, device_index)[None]


def solution(mesh):
    return jax.shard_map(
        on_device,
        mesh=mesh,
        in_specs=(
            P("pol", "fs", None, None),
            P(),
            P(),
            P(None, "fs", None, None),
            P("fs", None, None, None),
            P(),
        ),
        out_specs=P("pol", None, "fs", None, None),
        check_vma=False,
    )
```

time: 131 us -> 76.7 us (0.59)
  Pallas kernels: 115 us -> 68.9 us
  local copies, waits for them, and re-layouts: 14.4 us -> 6.49 us
    pallas_call x1, Pallas kernels: 44.7 us -> 20.5 us  [transform(): pl.pallas_call(functools.partial(transform_kernel, device_count), out_sha...]
    pallas_call x1, Pallas kernels: 41.1 us -> 20.6 us  [predict(): pl.pallas_call(functools.partial(predict_kernel, facet_local), out_shape=...]
    unnamed x16, local copies, waits for them, and re-layouts: 11.7 us -> 4.94 us
    pallas_call x1, Pallas kernels: 4.55 us -> 2.75 us  [correct(): pl.pallas_call(correct_kernel, out_shape=jax.ShapeDtypeStruct((2, capacit...]
where the time goes in v1:
time: 76.7 us; the launch traced here: 76 us
  Pallas kernels  68.9 us (90%)
  local copies, waits for them, and re-layouts  6.49 us (8%)
    pallas_call x1, Pallas kernels, add_up(): pl.pallas_call(functools.partial(add_up_kernel, device_count, pols), out_...  25.1 us
    pallas_call x1, Pallas kernels, predict(): pl.pallas_call(functools.partial(predict_kernel, facet_local), out_shape=...  20.6 us
    pallas_call x1, Pallas kernels, transform(): pl.pallas_call(functools.partial(transform_kernel, device_count), out_sha...  20.5 us
    unnamed x16, local copies, waits for them, and re-layouts  4.94 us
    pallas_call x1, Pallas kernels, correct(): pl.pallas_call(correct_kernel, out_shape=jax.ShapeDtypeStruct((2, capacit...  2.75 us

profile of v1, /device:TPU:11, one launch (start us, length us, event | category | flops | bytes accessed | tf_op | source)
XLA Modules:
  0.0 76.0 jit_solution(13596783513574735674)
XLA Ops:
  0.0 0.8 %constant_dynamic-slice_fusion.1 = (f32[4,512]{1,0:T(4,128)S(1)}, f32[4,512]{1,0:T(4,128)S(1)}) fusion(f32[8,512]{1,0:T(8,128)} %param.14, s32[]{:T(128)S(6)} %select_n.18, s32[]{:T(128)S(6)} %select_n.20), kind=kLoop, calls=%fused_computation.2 | loop fusion | bytes 32776 | tf_op jit(solution)/shard_map/dynamic_slice | solution.py:589
  0.8 0.6 pad_maximum_fusion.table_ref
  1.4 0.0 copy-start.3
  1.4 0.9 %copy-done.3 = f32[2,16,8,128]{3,2,1,0:T(8,128)S(1)} copy-done((f32[2,16,8,128]{3,2,1,0:T(8,128)S(1)}, f32[2,16,8,128]{3,2,1,0:T(8,128)}, u32[]{:S(2)}) %copy-start.3) | copy-done | bytes 131096
  2.3 0.0 copy-start.4
  2.3 1.6 %copy-done.4 = bf16[64,128,128]{2,1,0:T(8,128)(2,1)S(1)} copy-done((bf16[64,128,128]{2,1,0:T(8,128)(2,1)S(1)}, bf16[64,128,128]{2,1,0:T(8,128)(2,1)}, u32[]{:S(2)}) %copy-start.4) | copy-done | bytes 2097176
  3.9 0.0 copy-start.5
  3.9 0.9 %copy-done.5 = bf16[256,256]{1,0:T(8,128)(2,1)S(1)} copy-done((bf16[256,256]{1,0:T(8,128)(2,1)S(1)}, bf16[256,256]{1,0:T(8,128)(2,1)}, u32[]{:S(2)}) %copy-start.5) | copy-done | bytes 131096
  4.8 0.0 copy-start.6
  4.8 0.8 copy-done.6
  5.6 0.0 copy-start.1
  5.6 0.0 copy-start.2
  5.6 20.5 %shard_map.91 = (bf16[64,256,256]{2,1,0:T(8,128)(2,1)S(1)}, f32[8,2,16,8,128]{4,3,2,1,0:T(8,128)S(1)}) custom-call(bf16[8,4096,128]{2,1,0:T(8,128)(2,1)} %bitcast.11, bf16[64,128,128]{2,1,0:T(8,128)(2,1)S(1)} %copy-done.4, f32[2,16,8,128]{3,2,1,0:T(8,128)S(1)} %copy-done.3, bf16[256,256]{1,0:T(8,128)(2,1)S(1)} %copy-done.5, bf16[128,128]{1,0:T(8,128)(2,1)S(1)} %copy-done.6), custom_call_target="tpu_custom_call" | custom-call | flops 5000000000 | bytes 16777216 | tf_op jit(solution)/shard_map/pallas_call | solution.py:275
  26.1 0.0 copy-start.7
  26.1 0.0 copy-done.1
  26.1 0.0 copy-done.2
  26.1 20.6 %shard_map.92.in_ref = bf16[8,16,2,8,128]{4,3,2,1,0:T(8,128)(2,1)S(1)} custom-call(s32[1]{0:T(128)} %bitcast.index_ref, s32[64]{0:T(128)S(1)} %copy-done.1, s32[64]{0:T(128)S(1)} %copy-done.2, f32[8,2,16,8,128]{4,3,2,1,0:T(8,128)S(1)} %get-tuple-element.7.coords_ref, bf16[64,256,256]{2,1,0:T(8,128)(2,1)S(1)} %get-tuple-element.8.windows_ref), custom_call_target="tpu_custom_call" | custom-call | tf_op jit(solution)/shard_map/pallas_call | solution.py:421
  46.7 0.0 copy-start
  46.7 0.8 %copy-done = bf16[8,16,2,8,128]{4,3,2,1,0:T(8,128)(2,1)} copy-done((bf16[8,16,2,8,128]{4,3,2,1,0:T(8,128)(2,1)}, bf16[8,16,2,8,128]{4,3,2,1,0:T(8,128)(2,1)S(1)}, u32[]{:S(2)}) %copy-start) | copy-done | bytes 524312
  47.4 25.1 %shard_map.93.vis_ref = f32[4,16,2,8,128]{4,3,2,1,0:T(8,128)} custom-call(bf16[8,16,2,8,128]{4,3,2,1,0:T(8,128)(2,1)} %copy-done), custom_call_target="tpu_custom_call" | custom-call | tf_op jit(solution)/shard_map/pallas_call | solution.py:489
  72.5 0.0 copy-done.7
  72.5 0.7 fusion
  73.3 2.8 %shard_map.94 = f32[2,16,8,128]{3,2,1,0:T(8,128)} custom-call(s32[1]{0:T(128)} %bitcast.index_ref, s32[64]{0:T(128)} %owners_ref.3, s32[64]{0:T(128)} %counts_ref.3, s32[16,8,128]{2,1,0:T(8,128)} %bitcast.10, s32[16,8,128]{2,1,0:T(8,128)} %bitcast.9, f32[8,512]{1,0:T(8,128)} %pad_maximum_fusion.table_ref, f32[4,16,2,8,128]{4,3,2,1,0:T(8,128)} %shard_map.93.vis_ref), custom_call_target="tpu_custom_call" | custom-call | tf_op jit(solution)/shard_map/pallas_call | solution.py:564
Async XLA Ops:
  1.4 0.9 %copy-start.3 = (f32[2,16,8,128]{3,2,1,0:T(8,128)S(1)}, f32[2,16,8,128]{3,2,1,0:T(8,128)}, u32[]{:S(2)}) copy-start(f32[2,16,8,128]{3,2,1,0:T(8,128)} %coords_ref.1) | copy-start | bytes 393220
  2.3 1.6 %copy-start.4 = (bf16[64,128,128]{2,1,0:T(8,128)(2,1)S(1)}, bf16[64,128,128]{2,1,0:T(8,128)(2,1)}, u32[]{:S(2)}) copy-start(bf16[64,128,128]{2,1,0:T(8,128)(2,1)} %constant.44.clone.first_hbm) | copy-start | bytes 6291460
  3.9 0.9 %copy-start.5 = (bf16[256,256]{1,0:T(8,128)(2,1)S(1)}, bf16[256,256]{1,0:T(8,128)(2,1)}, u32[]{:S(2)}) copy-start(bf16[256,256]{1,0:T(8,128)(2,1)} %constant.45.clone.mix_ref) | copy-start | bytes 393220
  4.8 0.8 copy-start.6
  5.6 20.5 %copy-start.1 = (s32[64]{0:T(128)S(1)}, s32[64]{0:T(128)}, u32[]{:S(2)}) copy-start(s32[64]{0:T(128)} %owners_ref.3) | copy-start | bytes 772
  5.6 20.5 %copy-start.2 = (s32[64]{0:T(128)S(1)}, s32[64]{0:T(128)}, u32[]{:S(2)}) copy-start(s32[64]{0:T(128)} %counts_ref.3) | copy-start | bytes 772
  26.1 46.5 %copy-start.7 = (s32[16,8,2,128]{3,2,1,0:T(2,128)S(1)}, s32[16,8,2,128]{3,2,1,0:T(2,128)}, u32[]{:S(2)}) copy-start(s32[16,8,2,128]{3,2,1,0:T(2,128)} %param.13) | copy-start | bytes 393220
  46.7 0.8 %copy-start = (bf16[8,16,2,8,128]{4,3,2,1,0:T(8,128)(2,1)}, bf16[8,16,2,8,128]{4,3,2,1,0:T(8,128)(2,1)S(1)}, u32[]{:S(2)}) copy-start(bf16[8,16,2,8,128]{4,3,2,1,0:T(8,128)(2,1)S(1)} %shard_map.92.in_ref) | copy-start | bytes 1572868

commit v2 on v1

--- a/solution.py
+++ b/solution.py
@@ -17,9 +17,11 @@
 LANES = 128
 SPAN = 4
 PITCH = 65
-CHUNK = 1024
-UNROLL = 8
+CHUNK = 2048
+UNROLL = 32
 PAIRS = 4
+VMEM_BYTES = 67043328
+SLACK = 13000 * 1024
 
 
 def fit(values, terms):
@@ -76,6 +78,11 @@
     return as_real(table) / (math.sqrt(FH) * SG)
 
 
+def transform_tables():
+    mix = mix_table().reshape(2, 2 * W, 2, 2 * W).transpose(0, 2, 1, 3).reshape(4, 2 * W, 2 * W)
+    return np.concatenate([first_tables(), second_table()[None], mix])
+
+
 def horner(coefs, square):
     total = jnp.full_like(square, coefs[-1])
     for coef in coefs[-2::-1]:
@@ -106,8 +113,8 @@
 
 
 def transform_kernel(
-    device_count, strips_ref, first_hbm, coords_ref, mix_ref, second_ref, out_ref, gathered_ref,
-    strip_ref, first_ref, mixed_ref, turned_ref, everyone_ref, strip_sem, first_sem, own_sem,
+    device_count, strips_ref, tables_hbm, coords_ref, out_ref, gathered_ref,
+    strip_ref, first_ref, mix_ref, second_ref, mixed_ref, turned_ref, everyone_ref, strip_sem, table_sem, own_sem,
     send_sem, recv_sem, pair_send_sem, pair_recv_sem
 ):
     me = lax.axis_index("fs")
@@ -128,13 +135,25 @@
         pltpu.make_async_copy(strips_ref.at[f], strip_ref.at[f], strip_sem.at[f])
         for f in range(facet_local)
     ]
-    for low, high in order:
+    own = pltpu.make_async_copy(coords_ref, everyone_ref.at[me], own_sem)
+    own.start()
+    tables = [
+        pltpu.make_async_copy(from_ref, to_ref, table_sem.at[i])
+        for i, (from_ref, to_ref) in enumerate(
+            [
+                (tables_hbm.at[pl.ds(S + 1, 4)], mix_ref),
+                (tables_hbm.at[pl.ds(0, S)], first_ref),
+                (tables_hbm.at[S], second_ref),
+            ]
+        )
+    ]
+    tables[0].start()
+    for i, (low, high) in enumerate(order):
         loads[low].start()
         loads[high].start()
-    tables = pltpu.make_async_copy(first_hbm, first_ref, first_sem)
-    tables.start()
-    own = pltpu.make_async_copy(coords_ref, everyone_ref.at[me], own_sem)
-    own.start()
+        if i == 0:
+            tables[1].start()
+            tables[2].start()
 
     barrier = pltpu.get_barrier_semaphore()
     for step in range(1, device_count):
@@ -161,6 +180,11 @@
         copy.start()
         sends.append(copy)
 
+    tables[0].wait()
+    mix = jnp.concatenate(
+        [jnp.concatenate([mix_ref[2 * i], mix_ref[2 * i + 1]], axis=1) for i in range(2)], axis=0
+    )
+
     def lanes(pieces):
         return jnp.concatenate(pieces, axis=1).astype(jnp.bfloat16)
 
@@ -170,11 +194,11 @@
             loads[low].wait()
             loads[high].wait()
 
-            def mix(i, carry, low=low, high=high, pair=pair):
+            def join(i, carry, low=low, high=high, pair=pair):
                 rows = pl.ds(pl.multiple_of(i * CHUNK, CHUNK), CHUNK)
                 both = jnp.dot(
                     jnp.concatenate([strip_ref[low, rows, :], strip_ref[high, rows, :]], axis=1),
-                    mix_ref[...],
+                    mix,
                     preferred_element_type=jnp.float32,
                 )
                 for t in range(CHUNK // W):
@@ -185,9 +209,10 @@
                         ]
                 return carry
 
-            lax.fori_loop(0, FH // CHUNK, mix, 0)
+            lax.fori_loop(0, FH // CHUNK, join, 0)
         if group == 0:
-            tables.wait()
+            tables[1].wait()
+            tables[2].wait()
 
         def put(to_ref, rows, product):
             for pair in range(pairs):
@@ -267,27 +292,29 @@
 
 def transform(strips, coords, device_count):
     vmem = pl.BlockSpec(memory_space=pltpu.VMEM)
-    anywhere = pl.BlockSpec(memory_space=pl.ANY)
+    hbm = pl.BlockSpec(memory_space=pltpu.HBM)
     facet_local = strips.shape[0]
     span = min(SPAN, facet_local)
     scratch = pltpu.VMEM((span, S * PITCH, LANES), jnp.float32)
-    constant = lambda table: jnp.asarray(table, jnp.bfloat16)
+    kept = S * facet_local * 2 * W * W * 2 + device_count * coords.size * 4 + SLACK
     return pl.pallas_call(
         functools.partial(transform_kernel, device_count),
         out_shape=[
             jax.ShapeDtypeStruct((S, facet_local // span * 2 * W, span * W), jnp.bfloat16),
             jax.ShapeDtypeStruct((device_count,) + coords.shape, jnp.float32),
         ],
-        in_specs=[anywhere, anywhere, anywhere, vmem, vmem],
+        in_specs=[hbm] * 3,
         out_specs=[vmem, vmem],
         scratch_shapes=[
             pltpu.VMEM((facet_local, FH, LANES), jnp.bfloat16),
             pltpu.VMEM((S, 2 * W, 2 * W), jnp.bfloat16),
+            pltpu.VMEM((4, 2 * W, 2 * W), jnp.bfloat16),
+            pltpu.VMEM((2 * S, 2 * S), jnp.bfloat16),
             scratch,
             scratch,
             pltpu.VMEM((device_count,) + coords.shape, jnp.float32),
             pltpu.SemaphoreType.DMA((facet_local,)),
-            pltpu.SemaphoreType.DMA,
+            pltpu.SemaphoreType.DMA((3,)),
             pltpu.SemaphoreType.DMA,
             pltpu.SemaphoreType.DMA((device_count - 1,)),
             pltpu.SemaphoreType.DMA((device_count - 1,)),
@@ -295,21 +322,31 @@
             pltpu.SemaphoreType.DMA((device_count - 1,)),
         ],
         compiler_params=pltpu.CompilerParams(
-            vmem_limit_bytes=42 * 2**20, collective_id=0, has_side_effects=True
+            vmem_limit_bytes=VMEM_BYTES - kept, collective_id=0, has_side_effects=True
         ),
         cost_estimate=pl.CostEstimate(
             flops=5 * 10**9, bytes_accessed=16 * 2**20, transcendentals=0
         ),
-    )(strips, constant(first_tables()), coords, constant(mix_table()), constant(second_table()))
+    )(
+        strips,
+        pltpu.with_memory_space_constraint(jnp.asarray(transform_tables(), jnp.bfloat16), pltpu.HBM),
+        pltpu.with_memory_space_constraint(coords, pltpu.HBM),
+    )
 
 
 def predict_kernel(
-    facet_local, index_ref, owners_ref, counts_ref, coords_ref, windows_ref, parts_ref, out_ref,
-    table_ref, row_ref, place_ref, loads_ref
+    facet_local, part, device_count, index_ref, owners_ref, counts_ref, coords_ref, windows_ref,
+    *refs
 ):
-    device_count = out_ref.shape[0]
-    lane = out_ref.shape[4]
+    if part == 1:
+        refs = refs[1:]
+    limit_ref, *refs = refs
+    parts_refs = refs[: device_count // 2]
+    out_ref, table_ref, row_ref, list_ref, place_ref, load_ref, loads_ref = refs[device_count // 2 :]
+    lane = out_ref.shape[3]
+    near = device_count // 2
     subgrids = owners_ref.shape[0]
+    capacity = parts_refs[0].shape[0]
     span = min(SPAN, facet_local)
     groups = facet_local // span
     steps = span // 2
@@ -324,33 +361,53 @@
     row_pick = jnp.where(ramp == 0.0, 0.0, jnp.where(ramp == 1.0, 8.0, row_middle)) * unit
     out_ref[...] = jnp.zeros_like(out_ref)
 
-    def clear(i, carry):
-        loads_ref[i] = 0
-        return carry
-
-    lax.fori_loop(0, device_count, clear, 0)
-
-    def rank(s, total):
+    def clear(ref):
+        def body(i, carry):
+            ref[i] = 0
+            return carry
+
+        lax.fori_loop(0, ref.shape[0], body, 0)
+
+    clear(loads_ref)
+    clear(limit_ref)
+    list_ref[0] = 0
+    me = index_ref[0]
+
+    def rank(s, carry):
+        listed, total = carry
         owner = owners_ref[s]
         load = loads_ref[owner]
         loads_ref[owner] = load + 1
-        place_ref[s] = load
-        return total + lax.div(counts_ref[s] + 1, 2)
-
-    total = lax.fori_loop(0, subgrids, rank, 0)
-
-    def following(s, b):
+        count = counts_ref[s]
+        offset = owner ^ me
+        load_ref[s] = load
+        place_ref[s] = (offset - (1 - part) * near) * capacity + load
+        taken = jnp.where((offset >= near) == (part == 0), 1, 0)
+        list_ref[listed] = s
+
+        @pl.when(owner == me)
+        def _():
+            limit_ref[load] = count
+
+        return listed + taken, total + taken * lax.div(count + 1, 2)
+
+    listed, total = lax.fori_loop(0, subgrids, rank, (0, 0))
+    last = jnp.maximum(listed - 1, 0)
+    list_ref[listed] = list_ref[last]
+
+    def following(i, b):
         items = []
         for _ in range(PAIRS):
+            s = list_ref[i]
             items.append((s, b))
             done = b + 2 >= counts_ref[s]
-            end = jnp.logical_and(done, s == subgrids - 1)
+            end = jnp.logical_and(done, i == last)
             b = jnp.where(end, b, jnp.where(done, 0, b + 2))
-            s = jnp.where(done, jnp.minimum(s + 1, subgrids - 1), s)
-        return items, (s, b)
+            i = jnp.where(done, jnp.minimum(i + 1, last), i)
+        return items, (i, b)
 
     def tables(u, turn, s, b):
-        owner, load = owners_ref[s], place_ref[s]
+        owner, load = owners_ref[s], load_ref[s]
         for h in range(2):
             x = coords_ref[owner, 0, load, pl.ds(b + h, 1), :]
             y = coords_ref[owner, 1, load, pl.ds(b + h, 1), :]
@@ -373,7 +430,7 @@
 
     def predict(u, turn, s, b):
         grid = jnp.dot(windows_ref[s], table_ref[u], preferred_element_type=jnp.float32)
-        owner, load = owners_ref[s], place_ref[s]
+        place = place_ref[s]
         for h in range(2):
             real = imag = None
             for g in range(groups):
@@ -393,8 +450,8 @@
                 more_imag = sums[1] * cos - sums[0] * sin
                 real = more_real if real is None else real + more_real
                 imag = more_imag if imag is None else imag + more_imag
-            out_ref[owner, load, 0, pl.ds(b + h, 1), :] = jnp.sum(real, axis=0, keepdims=True)
-            out_ref[owner, load, 1, pl.ds(b + h, 1), :] = jnp.sum(imag, axis=0, keepdims=True)
+            out_ref[place, 0, pl.ds(b + h, 1), :] = jnp.sum(real, axis=0, keepdims=True)
+            out_ref[place, 1, pl.ds(b + h, 1), :] = jnp.sum(imag, axis=0, keepdims=True)
 
     items, after = following(0, 0)
     for u, (s, b) in enumerate(items):
@@ -410,48 +467,80 @@
         return items, after
 
     lax.fori_loop(0, lax.div(total + PAIRS - 1, PAIRS), step, (items, after))
-    parts_ref[...] = out_ref[...].astype(jnp.bfloat16)
-
-
-def predict(windows, owners, counts, coords, device_index, facet_local):
+    for i, parts_ref in enumerate(parts_refs):
+        parts_ref[...] = out_ref[i * capacity : (i + 1) * capacity].astype(jnp.bfloat16)
+
+
+def predict(windows, owners, counts, coords, device_index, facet_local, before=()):
     device_count, _, capacity, max_blocks, lane = coords.shape
     smem = pl.BlockSpec(memory_space=pltpu.SMEM)
     vmem = pl.BlockSpec(memory_space=pltpu.VMEM)
-    slots = (device_count, capacity, 2, max_blocks, lane)
-    return pl.pallas_call(
-        functools.partial(predict_kernel, facet_local),
-        out_shape=jax.ShapeDtypeStruct(slots, jnp.bfloat16),
-        in_specs=[smem, smem, smem, vmem, vmem],
-        out_specs=vmem,
+    near = device_count // 2
+    slots = (capacity, 2, max_blocks, lane)
+    part = len(before)
+    limit, *parts = pl.pallas_call(
+        functools.partial(predict_kernel, facet_local, part, device_count),
+        out_shape=[jax.ShapeDtypeStruct((capacity,), jnp.int32)]
+        + [jax.ShapeDtypeStruct(slots, jnp.bfloat16)] * near,
+        in_specs=[smem, smem, smem, vmem, vmem] + [smem] * part,
+        out_specs=[smem] + [vmem] * near,
         scratch_shapes=[
-            pltpu.VMEM(slots, jnp.float32),
+            pltpu.VMEM((near * capacity,) + slots[1:], jnp.float32),
             pltpu.VMEM((PAIRS, windows.shape[2], 2 * lane), jnp.bfloat16),
             pltpu.VMEM((2, PAIRS, 2, W + 16, lane), jnp.float32),
+            pltpu.SMEM((owners.shape[0] + 1,), jnp.int32),
+            pltpu.SMEM((owners.shape[0],), jnp.int32),
             pltpu.SMEM((owners.shape[0],), jnp.int32),
             pltpu.SMEM((device_count,), jnp.int32),
         ],
         compiler_params=pltpu.CompilerParams(vmem_limit_bytes=16 * 2**20),
-    )(device_index.reshape(1), owners, counts, coords, windows)
-
-
-def add_up_kernel(
-    device_count, pols, in_ref, out_ref, arrived_ref, total_ref, send_sem, recv_sem, pol_send_sem,
-    pol_recv_sem
-):
+        cost_estimate=pl.CostEstimate(
+            flops=2 * 10**10, bytes_accessed=2**20, transcendentals=0
+        ),
+    )(device_index.reshape(1), owners, counts, coords, windows, *before)
+    return limit, parts
+
+
+def flip(index, mask):
+    bit = 1
+    flipped = index
+    while bit <= mask:
+        if mask & bit:
+            flipped = flipped + bit * (1 - 2 * lax.rem(lax.div(index, bit), 2))
+        bit *= 2
+    return flipped
+
+
+def finish_kernel(near, pols, limit_ref, stations_hbm, table_ref, *refs):
+    near_refs = refs[:near]
+    far_refs = refs[near : 2 * near]
+    (
+        out_ref, far_ref, arrived_ref, station_ref, rows_ref, jones_ref, total_ref, sent_ref,
+        far_sem, station_sem, send_sem, recv_sem, pol_send_sem, pol_recv_sem
+    ) = refs[2 * near :]
     me = lax.axis_index("fs")
     pol = lax.axis_index("pol")
-    peers = [{"fs": lax.rem(me + step, device_count)} for step in range(1, device_count)]
+    capacity, _, max_blocks, lane = total_ref.shape
+    peers = [{"fs": flip(me, mask)} for mask in range(1, near)]
     pol_peers = [{"pol": lax.rem(pol + step, pols)} for step in range(1, pols)]
+    loads = [
+        pltpu.make_async_copy(from_ref, far_ref.at[i], far_sem.at[i])
+        for i, from_ref in enumerate(far_refs)
+    ]
+    stations = pltpu.make_async_copy(stations_hbm, station_ref, station_sem)
+    for load in loads:
+        load.start()
+    stations.start()
     barrier = pltpu.get_barrier_semaphore()
     for peer in peers + pol_peers:
         pl.semaphore_signal(
             barrier, inc=1, device_id=peer, device_id_type=pl.DeviceIdType.MESH
         )
-    pl.semaphore_wait(barrier, device_count + pols - 2)
+    pl.semaphore_wait(barrier, near + pols - 2)
     copies = []
     for i, peer in enumerate(peers):
         copy = pltpu.make_async_remote_copy(
-            src_ref=in_ref.at[peer["fs"]],
+            src_ref=near_refs[i + 1],
             dst_ref=arrived_ref.at[i],
             send_sem=send_sem.at[i],
             recv_sem=recv_sem.at[i],
@@ -460,15 +549,20 @@
         )
         copy.start()
         copies.append(copy)
-    total_ref[pol] = in_ref[me].astype(jnp.float32)
+    total = near_refs[0][...].astype(jnp.float32)
+    for i, load in enumerate(loads):
+        load.wait()
+        total = total + far_ref[i].astype(jnp.float32)
+    total_ref[...] = total
     for i, copy in enumerate(copies):
         copy.wait_recv()
-        total_ref[pol] += arrived_ref[i].astype(jnp.float32)
+        total_ref[...] += arrived_ref[i].astype(jnp.float32)
+    sent_ref[pol] = total_ref[...].astype(jnp.bfloat16)
     pol_copies = []
     for i, peer in enumerate(pol_peers):
         copy = pltpu.make_async_remote_copy(
-            src_ref=total_ref.at[pol],
-            dst_ref=total_ref.at[pol],
+            src_ref=sent_ref.at[pol],
+            dst_ref=sent_ref.at[pol],
             send_sem=pol_send_sem.at[i],
             recv_sem=pol_recv_sem.at[i],
             device_id=peer,
@@ -476,122 +570,120 @@
         )
         copy.start()
         pol_copies.append(copy)
+    stations.wait()
+    chunks = table_ref.shape[1] // lane
+    firsts = [4 * lax.div(pol, 2), 4 * lax.rem(pol, 2)]
+    for row in range(table_ref.shape[0]):
+        for chunk in range(chunks):
+            at = row * chunks + chunk
+            rows_ref[at : at + 1, :] = table_ref[row : row + 1, chunk * lane : (chunk + 1) * lane]
+
+    def look_up(load, carry):
+        for side in range(2):
+            ids = station_ref[load, pl.ds(side, max_blocks, stride=2), :]
+            low = ids & (lane - 1)
+            high = ids >> (lane.bit_length() - 1)
+            for row in range(4):
+                entry = None
+                for chunk in range(chunks):
+                    source = jnp.broadcast_to(
+                        rows_ref[pl.ds((firsts[side] + row) * chunks + chunk, 1), :],
+                        (max_blocks, lane),
+                    )
+                    got = jnp.take_along_axis(source, low, axis=1, mode="promise_in_bounds")
+                    entry = got if entry is None else jnp.where(high == chunk, got, entry)
+                jones_ref[load, 4 * side + row] = entry
+        return carry
+
+    lax.fori_loop(0, capacity, look_up, 0)
     for copy in pol_copies:
         copy.wait_recv()
+    block = lax.broadcasted_iota(jnp.int32, (max_blocks, lane), 0)
+
+    def product(a, b):
+        return (a[0] * b[0] - a[1] * b[1], a[0] * b[1] + a[1] * b[0])
+
+    def correct(load, carry):
+        jones = [jones_ref[load, i] for i in range(8)]
+        real = jnp.zeros((max_blocks, lane), jnp.float32)
+        imag = jnp.zeros((max_blocks, lane), jnp.float32)
+        for row in range(2):
+            for col in range(2):
+                comp = 2 * row + col
+                visible = [
+                    jnp.where(
+                        pol == comp, total_ref[load, i], sent_ref[comp, load, i].astype(jnp.float32)
+                    )
+                    for i in range(2)
+                ]
+                step = product((jones[2 * row], jones[2 * row + 1]), visible)
+                step = product(step, (jones[4 + 2 * col], -jones[5 + 2 * col]))
+                real = real + step[0]
+                imag = imag + step[1]
+        keep = block < limit_ref[load]
+        out_ref[0, load] = jnp.where(keep, real, 0.0)
+        out_ref[1, load] = jnp.where(keep, imag, 0.0)
+        return carry
+
+    lax.fori_loop(0, capacity, correct, 0)
     for copy in copies + pol_copies:
         copy.wait_send()
-    out_ref[...] = total_ref[...]
-
-
-def add_up(parts, pols):
-    device_count = parts.shape[0]
+
+
+def finish(limit, near_parts, far_parts, station_ids, table, pols):
+    near = len(near_parts)
+    slots = near_parts[0].shape
+    capacity, _, max_blocks, lane = slots
+    smem = pl.BlockSpec(memory_space=pltpu.SMEM)
     vmem = pl.BlockSpec(memory_space=pltpu.VMEM)
+    hbm = pl.BlockSpec(memory_space=pltpu.HBM)
+    anywhere = pl.BlockSpec(memory_space=pl.ANY)
     return pl.pallas_call(
-        functools.partial(add_up_kernel, device_count, pols),
-        out_shape=jax.ShapeDtypeStruct((pols,) + parts.shape[1:], jnp.float32),
-        in_specs=[vmem],
+        functools.partial(finish_kernel, near, pols),
+        out_shape=jax.ShapeDtypeStruct((2, capacity, max_blocks, lane), jnp.float32),
+        in_specs=[smem, hbm, vmem] + [vmem] * near + [anywhere] * near,
         out_specs=vmem,
         scratch_shapes=[
-            pltpu.VMEM((device_count - 1,) + parts.shape[1:], jnp.bfloat16),
-            pltpu.VMEM((pols,) + parts.shape[1:], jnp.float32),
-            pltpu.SemaphoreType.DMA((device_count - 1,)),
-            pltpu.SemaphoreType.DMA((device_count - 1,)),
+            pltpu.VMEM((near,) + slots, jnp.bfloat16),
+            pltpu.VMEM((near - 1,) + slots, jnp.bfloat16),
+            pltpu.VMEM((capacity, 2 * max_blocks, lane), jnp.int32),
+            pltpu.VMEM((table.size // lane, lane), jnp.float32),
+            pltpu.VMEM((capacity, 8, max_blocks, lane), jnp.float32),
+            pltpu.VMEM(slots, jnp.float32),
+            pltpu.VMEM((pols,) + slots, jnp.bfloat16),
+            pltpu.SemaphoreType.DMA((near,)),
+            pltpu.SemaphoreType.DMA,
+            pltpu.SemaphoreType.DMA((near - 1,)),
+            pltpu.SemaphoreType.DMA((near - 1,)),
             pltpu.SemaphoreType.DMA((pols - 1,)),
             pltpu.SemaphoreType.DMA((pols - 1,)),
         ],
-        compiler_params=pltpu.CompilerParams(collective_id=1, has_side_effects=True),
-    )(parts)
-
-
-def correct_kernel(index_ref, owners_ref, counts_ref, left_ref, right_ref, table_ref, vis_ref, out_ref):
-    capacity = out_ref.shape[1]
-    max_blocks, lane = out_ref.shape[2:]
-    chunks = table_ref.shape[1] // lane
-    me = index_ref[0]
-    out_ref[...] = jnp.zeros_like(out_ref)
-    block = lax.broadcasted_iota(jnp.int32, (max_blocks, lane), 0)
-
-    def look_up(first, ids):
-        low = ids % lane
-        high = ids // lane
-        found = []
-        for row in range(4):
-            entry = None
-            for chunk in range(chunks):
-                source = jnp.broadcast_to(
-                    table_ref[first + row : first + row + 1, chunk * lane : (chunk + 1) * lane],
-                    (max_blocks, lane),
-                )
-                got = jnp.take_along_axis(source, low, axis=1, mode="promise_in_bounds")
-                entry = got if entry is None else jnp.where(high == chunk, got, entry)
-            found.append(entry)
-        return [(found[0], found[1]), (found[2], found[3])]
-
-    def product(a, b):
-        return (a[0] * b[0] - a[1] * b[1], a[0] * b[1] + a[1] * b[0])
-
-    def slot(s, load):
-        is_mine = owners_ref[s] == me
-
-        @pl.when(is_mine)
-        def _():
-            left = look_up(0, left_ref[load])
-            right = look_up(4, right_ref[load])
-            total_real = jnp.zeros((max_blocks, lane), jnp.float32)
-            total_imag = jnp.zeros((max_blocks, lane), jnp.float32)
-            for inner_row in range(2):
-                for inner_col in range(2):
-                    comp = 2 * inner_row + inner_col
-                    step = product(
-                        left[inner_row], (vis_ref[comp, load, 0], vis_ref[comp, load, 1])
-                    )
-                    step = product(step, (right[inner_col][0], -right[inner_col][1]))
-                    total_real = total_real + step[0]
-                    total_imag = total_imag + step[1]
-            keep = block < counts_ref[s]
-            out_ref[0, load] = jnp.where(keep, total_real, 0.0)
-            out_ref[1, load] = jnp.where(keep, total_imag, 0.0)
-
-        return load + is_mine.astype(jnp.int32)
-
-    lax.fori_loop(0, owners_ref.shape[0], slot, 0)
-
-
-def correct(visible, owners, counts, station_ids, tables, device_index):
-    _, capacity, _, max_blocks, lane = visible.shape
-    smem = pl.BlockSpec(memory_space=pltpu.SMEM)
-    vmem = pl.BlockSpec(memory_space=pltpu.VMEM)
-    return pl.pallas_call(
-        correct_kernel,
-        out_shape=jax.ShapeDtypeStruct((2, capacity, max_blocks, lane), jnp.float32),
-        in_specs=[smem, smem, smem, vmem, vmem, vmem, vmem],
-        out_specs=vmem,
+        compiler_params=pltpu.CompilerParams(
+            vmem_limit_bytes=8 * 2**20, collective_id=1, has_side_effects=True
+        ),
     )(
-        device_index.reshape(1),
-        owners,
-        counts,
-        station_ids[:, :, 0, :],
-        station_ids[:, :, 1, :],
-        tables,
-        visible,
+        limit,
+        station_ids.reshape(capacity, 2 * max_blocks, lane),
+        table,
+        *near_parts,
+        *far_parts,
     )
 
 
 def on_device(facets, owners, counts, coords, station_ids, jones_table):
     device_index = lax.axis_index("fs").astype(jnp.int32)
-    pol_index = lax.axis_index("pol")
     device_count, pols = lax.axis_size("fs"), lax.axis_size("pol")
     windows, all_coords = transform(facets[0], coords, device_count)
-    parts = predict(windows, owners, counts, all_coords, device_index, facets.shape[1])
-    visible = add_up(parts, pols)
-    tables = jnp.concatenate(
-        [
-            lax.dynamic_slice_in_dim(jones_table, 4 * (pol_index // 2), 4, 0),
-            lax.dynamic_slice_in_dim(jones_table, 4 * (pol_index % 2), 4, 0),
-        ],
-        axis=0,
+    near = device_count // 2
+    first, parts = predict(windows, owners, counts, all_coords, device_index, facets.shape[1])
+    far_parts = [
+        lax.ppermute(part, "fs", [(i, i ^ (near + mask)) for i in range(device_count)])
+        for mask, part in enumerate(parts)
+    ]
+    limit, near_parts = predict(
+        windows, owners, counts, all_coords, device_index, facets.shape[1], (first,)
     )
-    return correct(visible, owners, counts, station_ids, tables, device_index)[None]
+    return finish(limit, near_parts, far_parts, station_ids, jones_table, pols)[None]
 
 
 def solution(mesh):

time: 76.7 us -> 72.1 us (0.940)
  the two profiles are of different devices: /device:TPU:11 before, /device:TPU:1 now
where the time goes in v2:
time: 72.1 us; the launch traced here: 73.5 us
  Pallas kernels  54.5 us (76%)
  starting transfers between devices  18.2 us (25%)
    pallas_call x2, Pallas kernels, predict(): pl.pallas_call(functools.partial(predict_kernel, facet_local, part, devic...  23.4 us
    pallas_call x1, Pallas kernels, transform(): pl.pallas_call(functools.partial(transform_kernel, device_count), out_sha...  18.9 us
    ppermute x4, starting transfers between devices, on_device(): lax.ppermute(part, 'fs', [(i, i ^ near + mask) for i in range(device_coun...  18.2 us
    pallas_call x1, Pallas kernels, finish(): pl.pallas_call(functools.partial(finish_kernel, near, pols), out_shape=ja...  12.2 us
  transfers between devices with their start and end apart: 4, of which 0 were waited for; matrix products, arithmetic and copies ran while one was open for 0% of the time, Pallas kernels for 24%

profile of v2, /device:TPU:1, one launch (start us, length us, event | category | flops | bytes accessed | tf_op | source)
XLA Modules:
  0.0 73.5 jit_solution(3099435971812269550)
XLA Ops:
  0.0 0.0 copy-start.2
  0.0 0.0 copy-start.3
  0.0 18.9 %shard_map.73 = (bf16[64,256,256]{2,1,0:T(8,128)(2,1)S(1)}, f32[8,2,16,8,128]{4,3,2,1,0:T(8,128)S(1)}) custom-call(bf16[8,4096,128]{2,1,0:T(8,128)(2,1)} %bitcast.6, bf16[69,128,128]{2,1,0:T(8,128)(2,1)} %constant.8.clone.tables_hbm, f32[2,16,8,128]{3,2,1,0:T(8,128)} %coords_ref.1), custom_call_target="tpu_custom_call" | custom-call | flops 5000000000 | bytes 16777216 | tf_op jit(solution)/shard_map/pallas_call | solution.py:300
  18.9 0.0 copy-done.2
  18.9 0.0 copy-done.3
  19.0 6.1 %shard_map.74 = (s32[16]{0:T(128)S(1)}, bf16[16,2,8,128]{3,2,1,0:T(8,128)(2,1)S(1)}, bf16[16,2,8,128]{3,2,1,0:T(8,128)(2,1)S(1)}, bf16[16,2,8,128]{3,2,1,0:T(8,128)(2,1)S(1)}, bf16[16,2,8,128]{3,2,1,0:T(8,128)(2,1)S(1)}) custom-call(s32[1]{0:T(128)} %bitcast.index_ref, s32[64]{0:T(128)S(1)} %copy-done.2, s32[64]{0:T(128)S(1)} %copy-done.3, ...), custom_call_target="tpu_custom_call" | custom-call | flops 20000000000 | bytes 1048576 | tf_op jit(solution)/shard_map/pallas_call | solution.py:481
  25.1 12.2 %collective-permute-start = (bf16[16,2,8,128]{3,2,1,0:T(8,128)(2,1)S(1)}, bf16[16,2,8,128]{3,2,1,0:T(8,128)(2,1)S(1)}, u32[]{:S(2)}, u32[]{:S(2)}) collective-permute-start(bf16[16,2,8,128]{3,2,1,0:T(8,128)(2,1)S(1)} %get-tuple-element.25), channel_id=1, source_target_pairs={{0,16},{4,20},{8,24},{12,28},{16,0},{20,4},{24,8},{28,12},{1,17},{... | collective-permute-start | bytes 196616 | tf_op jit(solution)/shard_map/ppermute | solution.py:680
  37.3 0.8 %collective-permute-start.1 = (bf16[16,2,8,128]{3,2,1,0:T(8,128)(2,1)S(1)}, bf16[16,2,8,128]{3,2,1,0:T(8,128)(2,1)S(1)}, u32[]{:S(2)}, u32[]{:S(2)}) collective-permute-start(bf16[16,2,8,128]{3,2,1,0:T(8,128)(2,1)S(1)} %get-tuple-element.26), channel_id=1, source_target_pairs={{0,20},{4,16},{8,28},{12,24},{16,4},{20,0},{24,12},{28,8},{1,21},{... | collective-permute-start | bytes 196616 | tf_op jit(solution)/shard_map/ppermute | solution.py:680
  38.1 4.9 %collective-permute-start.2 = (bf16[16,2,8,128]{3,2,1,0:T(8,128)(2,1)S(1)}, bf16[16,2,8,128]{3,2,1,0:T(8,128)(2,1)S(1)}, u32[]{:S(2)}, u32[]{:S(2)}) collective-permute-start(bf16[16,2,8,128]{3,2,1,0:T(8,128)(2,1)S(1)} %get-tuple-element.27), channel_id=1, source_target_pairs={{0,24},{4,28},{8,16},{12,20},{16,8},{20,12},{24,0},{28,4},{1,25},{... | collective-permute-start | bytes 196616 | tf_op jit(solution)/shard_map/ppermute | solution.py:680
  43.0 0.3 collective-permute-start.3
  43.3 0.0 copy-start
  43.3 0.0 copy-start.1
  43.3 17.3 %shard_map.75 = (s32[16]{0:T(128)S(1)}, bf16[16,2,8,128]{3,2,1,0:T(8,128)(2,1)S(1)}, bf16[16,2,8,128]{3,2,1,0:T(8,128)(2,1)S(1)}, bf16[16,2,8,128]{3,2,1,0:T(8,128)(2,1)S(1)}, bf16[16,2,8,128]{3,2,1,0:T(8,128)(2,1)S(1)}) custom-call(s32[1]{0:T(128)} %bitcast.index_ref, s32[64]{0:T(128)S(1)} %copy-done.2, s32[64]{0:T(128)S(1)} %copy-done.3, ...), custom_call_target="tpu_custom_call" | custom-call | flops 20000000000 | bytes 1048576 | tf_op jit(solution)/shard_map/pallas_call | solution.py:481
  60.6 0.0 collective-permute-done.refs_4_
  60.6 0.0 collective-permute-done.1.refs_5_
  60.6 0.0 collective-permute-done.2.refs_6_
  60.7 0.0 collective-permute-done.3.refs_7_
  60.7 0.0 copy-done
  60.7 0.0 copy-done.1
  60.7 12.2 %shard_map.76 = f32[2,16,8,128]{3,2,1,0:T(8,128)S(1)} custom-call(s32[16]{0:T(128)S(1)} %get-tuple-element.20.limit_ref, s32[16,16,128]{2,1,0:T(8,128)S(1)} %bitcast.5, f32[8,512]{1,0:T(8,128)S(1)} %copy-done.1, bf16[16,2,8,128]{3,2,1,0:T(8,128)(2,1)S(1)} %get-tuple-element.21.refs_0_, bf16[16,2,8,128]{3,2,1,0:T(8,128)(2,1)S(1)} %get-tuple-element.22.refs_1_, ...), custom_call_target="tpu_custom_call" | custom-call | tf_op jit(solution)/shard_map/pallas_call | solution.py:641
  72.9 0.7 copy.9
Async XLA Ops:
  0.0 18.9 %copy-start.2 = (s32[64]{0:T(128)S(1)}, s32[64]{0:T(128)}, u32[]{:S(2)}) copy-start(s32[64]{0:T(128)} %owners_ref.3) | copy-start | bytes 772
  0.0 18.9 %copy-start.3 = (s32[64]{0:T(128)S(1)}, s32[64]{0:T(128)}, u32[]{:S(2)}) copy-start(s32[64]{0:T(128)} %counts_ref.3) | copy-start | bytes 772
  25.1 35.5 %collective-permute-start = (bf16[16,2,8,128]{3,2,1,0:T(8,128)(2,1)S(1)}, bf16[16,2,8,128]{3,2,1,0:T(8,128)(2,1)S(1)}, u32[]{:S(2)}, u32[]{:S(2)}) collective-permute-start(bf16[16,2,8,128]{3,2,1,0:T(8,128)(2,1)S(1)} %get-tuple-element.25), channel_id=1, source_target_pairs={{0,16},{4,20},{8,24},{12,28},{16,0},{20,4},{24,8},{28,12},{1,17},{... | collective-permute-start | bytes 196616 | tf_op jit(solution)/shard_map/ppermute | solution.py:680
  37.3 23.3 %collective-permute-start.1 = (bf16[16,2,8,128]{3,2,1,0:T(8,128)(2,1)S(1)}, bf16[16,2,8,128]{3,2,1,0:T(8,128)(2,1)S(1)}, u32[]{:S(2)}, u32[]{:S(2)}) collective-permute-start(bf16[16,2,8,128]{3,2,1,0:T(8,128)(2,1)S(1)} %get-tuple-element.26), channel_id=1, source_target_pairs={{0,20},{4,16},{8,28},{12,24},{16,4},{20,0},{24,12},{28,8},{1,21},{... | collective-permute-start | bytes 196616 | tf_op jit(solution)/shard_map/ppermute | solution.py:680
  38.1 22.6 %collective-permute-start.2 = (bf16[16,2,8,128]{3,2,1,0:T(8,128)(2,1)S(1)}, bf16[16,2,8,128]{3,2,1,0:T(8,128)(2,1)S(1)}, u32[]{:S(2)}, u32[]{:S(2)}) collective-permute-start(bf16[16,2,8,128]{3,2,1,0:T(8,128)(2,1)S(1)} %get-tuple-element.27), channel_id=1, source_target_pairs={{0,24},{4,28},{8,16},{12,20},{16,8},{20,12},{24,0},{28,4},{1,25},{... | collective-permute-start | bytes 196616 | tf_op jit(solution)/shard_map/ppermute | solution.py:680
  43.0 17.7 %collective-permute-start.3 = (bf16[16,2,8,128]{3,2,1,0:T(8,128)(2,1)S(1)}, bf16[16,2,8,128]{3,2,1,0:T(8,128)(2,1)S(1)}, u32[]{:S(2)}, u32[]{:S(2)}) collective-permute-start(bf16[16,2,8,128]{3,2,1,0:T(8,128)(2,1)S(1)} %get-tuple-element.28), channel_id=1, source_target_pairs={{0,28},{4,24},{8,20},{12,16},{16,12},{20,8},{24,4},{28,0},{1,29},{... | collective-permute-start | bytes 196616 | tf_op jit(solution)/shard_map/ppermute | solution.py:680
  43.3 17.4 %copy-start = (s32[16,8,2,128]{3,2,1,0:T(2,128)S(1)}, s32[16,8,2,128]{3,2,1,0:T(2,128)}, u32[]{:S(2)}) copy-start(s32[16,8,2,128]{3,2,1,0:T(2,128)} %param.11) | copy-start | bytes 393220
  43.3 17.4 %copy-start.1 = (f32[8,512]{1,0:T(8,128)S(1)}, f32[8,512]{1,0:T(8,128)}, u32[]{:S(2)}) copy-start(f32[8,512]{1,0:T(8,128)} %table_ref.1) | copy-start | bytes 49156

commit v3 on v2

--- a/solution.py
+++ b/solution.py
@@ -112,10 +112,20 @@
     return terms
 
 
+def flip(index, mask):
+    bit = 1
+    flipped = index
+    while bit <= mask:
+        if mask & bit:
+            flipped = flipped + bit * (1 - 2 * lax.rem(lax.div(index, bit), 2))
+        bit *= 2
+    return flipped
+
+
 def transform_kernel(
     device_count, strips_ref, tables_hbm, coords_ref, out_ref, gathered_ref,
     strip_ref, first_ref, mix_ref, second_ref, mixed_ref, turned_ref, everyone_ref, strip_sem, table_sem, own_sem,
-    send_sem, recv_sem, pair_send_sem, pair_recv_sem
+    pair_send_sem, pair_recv_sem, line_send_sem, line_recv_sem, core_send_sem, core_recv_sem
 ):
     me = lax.axis_index("fs")
     pol = lax.axis_index("pol")
@@ -155,30 +165,43 @@
             tables[1].start()
             tables[2].start()
 
+    across = {"fs": flip(me, 1)}
+    line = {h: {"fs": flip(me, 2 * h)} for h in range(1, device_count // 2)}
     barrier = pltpu.get_barrier_semaphore()
-    for step in range(1, device_count):
-        pl.semaphore_signal(
-            barrier,
-            inc=1,
-            device_id={"fs": lax.rem(me + step, device_count)},
-            device_id_type=pl.DeviceIdType.MESH,
-        )
-    pl.semaphore_signal(barrier, inc=1, device_id=partner, device_id_type=pl.DeviceIdType.MESH)
-    pl.semaphore_wait(barrier, device_count)
+    for peer in [partner, across] + list(line.values()):
+        pl.semaphore_signal(barrier, inc=1, device_id=peer, device_id_type=pl.DeviceIdType.MESH)
+    pl.semaphore_wait(barrier, device_count // 2 + 1)
     own.wait()
     sends = []
-    for step in range(1, device_count):
-        mine = everyone_ref.at[me, :, pl.ds(half * slots, slots)]
+
+    def send(source, peer, send_sem, recv_sem, index):
+        piece = everyone_ref.at[source, :, pl.ds(half * slots, slots)]
         copy = pltpu.make_async_remote_copy(
-            src_ref=mine,
-            dst_ref=mine,
-            send_sem=send_sem.at[step - 1],
-            recv_sem=recv_sem.at[step - 1],
-            device_id={"fs": lax.rem(me + step, device_count)},
+            src_ref=piece,
+            dst_ref=piece,
+            send_sem=send_sem.at[index],
+            recv_sem=recv_sem.at[index],
+            device_id=peer,
             device_id_type=pl.DeviceIdType.MESH,
         )
         copy.start()
         sends.append(copy)
+        return copy
+
+    def to_partner(mask):
+        return send(flip(me, mask), partner, core_send_sem, core_recv_sem, mask - 1)
+
+    crossed = {0: send(me, across, pair_send_sem, pair_recv_sem, 0)}
+    reached = {
+        h: send(me, line[h], line_send_sem, line_recv_sem, h - 1) for h in reversed(list(line))
+    }
+    handed = []
+
+    def relay(masks):
+        for h in masks:
+            reached[h].wait_recv()
+            crossed[h] = send(flip(me, 2 * h), across, pair_send_sem, pair_recv_sem, h)
+            handed.append(to_partner(2 * h))
 
     tables[0].wait()
     mix = jnp.concatenate(
@@ -242,6 +265,8 @@
             return carry
 
         lax.fori_loop(0, S // UNROLL, first, 0)
+        if group == 0:
+            relay([1])
 
         def second(i, carry):
             for u in range(UNROLL):
@@ -258,6 +283,8 @@
             return carry
 
         lax.fori_loop(0, W // UNROLL, second, 0)
+        if group == 0:
+            relay(range(2, device_count // 2))
 
         def third(i, carry, group=group):
             for u in range(2):
@@ -267,25 +294,12 @@
 
         lax.fori_loop(0, S // 2, third, 0)
 
-    forwards = []
-    for step in range(1, device_count):
-        sends[step - 1].wait_recv()
-        theirs = everyone_ref.at[
-            lax.rem(me + device_count - step, device_count), :, pl.ds(half * slots, slots)
-        ]
-        copy = pltpu.make_async_remote_copy(
-            src_ref=theirs,
-            dst_ref=theirs,
-            send_sem=pair_send_sem.at[step - 1],
-            recv_sem=pair_recv_sem.at[step - 1],
-            device_id=partner,
-            device_id_type=pl.DeviceIdType.MESH,
-        )
-        copy.start()
-        forwards.append(copy)
-    for copy in forwards:
+    for h in range(device_count // 2):
+        crossed[h].wait_recv()
+        handed.append(to_partner(2 * h + 1))
+    for copy in handed:
         copy.wait_recv()
-    for copy in sends + forwards:
+    for copy in sends:
         copy.wait_send()
     gathered_ref[...] = everyone_ref[...]
 
@@ -316,8 +330,10 @@
             pltpu.SemaphoreType.DMA((facet_local,)),
             pltpu.SemaphoreType.DMA((3,)),
             pltpu.SemaphoreType.DMA,
-            pltpu.SemaphoreType.DMA((device_count - 1,)),
-            pltpu.SemaphoreType.DMA((device_count - 1,)),
+            pltpu.SemaphoreType.DMA((device_count // 2,)),
+            pltpu.SemaphoreType.DMA((device_count // 2,)),
+            pltpu.SemaphoreType.DMA((device_count // 2 - 1,)),
+            pltpu.SemaphoreType.DMA((device_count // 2 - 1,)),
             pltpu.SemaphoreType.DMA((device_count - 1,)),
             pltpu.SemaphoreType.DMA((device_count - 1,)),
         ],
@@ -335,18 +351,13 @@
 
 
 def predict_kernel(
-    facet_local, part, device_count, index_ref, owners_ref, counts_ref, coords_ref, windows_ref,
-    *refs
+    facet_local, device_count, index_ref, owners_ref, counts_ref, coords_ref, windows_ref,
+    limit_ref, kept_ref, sent_ref, out_ref, table_ref, row_ref, place_ref, load_ref, loads_ref
 ):
-    if part == 1:
-        refs = refs[1:]
-    limit_ref, *refs = refs
-    parts_refs = refs[: device_count // 2]
-    out_ref, table_ref, row_ref, list_ref, place_ref, load_ref, loads_ref = refs[device_count // 2 :]
     lane = out_ref.shape[3]
-    near = device_count // 2
+    half = device_count // 2
     subgrids = owners_ref.shape[0]
-    capacity = parts_refs[0].shape[0]
+    capacity = kept_ref.shape[1]
     span = min(SPAN, facet_local)
     groups = facet_local // span
     steps = span // 2
@@ -370,41 +381,34 @@
 
     clear(loads_ref)
     clear(limit_ref)
-    list_ref[0] = 0
     me = index_ref[0]
 
-    def rank(s, carry):
-        listed, total = carry
+    def rank(s, total):
         owner = owners_ref[s]
         load = loads_ref[owner]
         loads_ref[owner] = load + 1
         count = counts_ref[s]
         offset = owner ^ me
         load_ref[s] = load
-        place_ref[s] = (offset - (1 - part) * near) * capacity + load
-        taken = jnp.where((offset >= near) == (part == 0), 1, 0)
-        list_ref[listed] = s
+        place_ref[s] = ((offset & 1) * half + (offset >> 1)) * capacity + load
 
         @pl.when(owner == me)
         def _():
             limit_ref[load] = count
 
-        return listed + taken, total + taken * lax.div(count + 1, 2)
-
-    listed, total = lax.fori_loop(0, subgrids, rank, (0, 0))
-    last = jnp.maximum(listed - 1, 0)
-    list_ref[listed] = list_ref[last]
-
-    def following(i, b):
+        return total + lax.div(count + 1, 2)
+
+    total = lax.fori_loop(0, subgrids, rank, 0)
+
+    def following(s, b):
         items = []
         for _ in range(PAIRS):
-            s = list_ref[i]
             items.append((s, b))
             done = b + 2 >= counts_ref[s]
-            end = jnp.logical_and(done, i == last)
+            end = jnp.logical_and(done, s == subgrids - 1)
             b = jnp.where(end, b, jnp.where(done, 0, b + 2))
-            i = jnp.where(done, jnp.minimum(i + 1, last), i)
-        return items, (i, b)
+            s = jnp.where(done, jnp.minimum(s + 1, subgrids - 1), s)
+        return items, (s, b)
 
     def tables(u, turn, s, b):
         owner, load = owners_ref[s], load_ref[s]
@@ -467,28 +471,29 @@
         return items, after
 
     lax.fori_loop(0, lax.div(total + PAIRS - 1, PAIRS), step, (items, after))
-    for i, parts_ref in enumerate(parts_refs):
-        parts_ref[...] = out_ref[i * capacity : (i + 1) * capacity].astype(jnp.bfloat16)
-
-
-def predict(windows, owners, counts, coords, device_index, facet_local, before=()):
+    kept_ref[...] = out_ref[: half * capacity].reshape(kept_ref.shape)
+    sent_ref[...] = out_ref[half * capacity :].reshape(sent_ref.shape).astype(jnp.bfloat16)
+
+
+def predict(windows, owners, counts, coords, device_index, facet_local):
     device_count, _, capacity, max_blocks, lane = coords.shape
     smem = pl.BlockSpec(memory_space=pltpu.SMEM)
     vmem = pl.BlockSpec(memory_space=pltpu.VMEM)
-    near = device_count // 2
     slots = (capacity, 2, max_blocks, lane)
-    part = len(before)
-    limit, *parts = pl.pallas_call(
-        functools.partial(predict_kernel, facet_local, part, device_count),
-        out_shape=[jax.ShapeDtypeStruct((capacity,), jnp.int32)]
-        + [jax.ShapeDtypeStruct(slots, jnp.bfloat16)] * near,
-        in_specs=[smem, smem, smem, vmem, vmem] + [smem] * part,
-        out_specs=[smem] + [vmem] * near,
+    half = (device_count // 2,) + slots
+    return pl.pallas_call(
+        functools.partial(predict_kernel, facet_local, device_count),
+        out_shape=[
+            jax.ShapeDtypeStruct((capacity,), jnp.int32),
+            jax.ShapeDtypeStruct(half, jnp.float32),
+            jax.ShapeDtypeStruct(half, jnp.bfloat16),
+        ],
+        in_specs=[smem, smem, smem, vmem, vmem],
+        out_specs=[smem, vmem, vmem],
         scratch_shapes=[
-            pltpu.VMEM((near * capacity,) + slots[1:], jnp.float32),
+            pltpu.VMEM((device_count * capacity,) + slots[1:], jnp.float32),
             pltpu.VMEM((PAIRS, windows.shape[2], 2 * lane), jnp.bfloat16),
             pltpu.VMEM((2, PAIRS, 2, W + 16, lane), jnp.float32),
-            pltpu.SMEM((owners.shape[0] + 1,), jnp.int32),
             pltpu.SMEM((owners.shape[0],), jnp.int32),
             pltpu.SMEM((owners.shape[0],), jnp.int32),
             pltpu.SMEM((device_count,), jnp.int32),
@@ -497,67 +502,63 @@
         cost_estimate=pl.CostEstimate(
             flops=2 * 10**10, bytes_accessed=2**20, transcendentals=0
         ),
-    )(device_index.reshape(1), owners, counts, coords, windows, *before)
-    return limit, parts
-
-
-def flip(index, mask):
-    bit = 1
-    flipped = index
-    while bit <= mask:
-        if mask & bit:
-            flipped = flipped + bit * (1 - 2 * lax.rem(lax.div(index, bit), 2))
-        bit *= 2
-    return flipped
-
-
-def finish_kernel(near, pols, limit_ref, stations_hbm, table_ref, *refs):
-    near_refs = refs[:near]
-    far_refs = refs[near : 2 * near]
-    (
-        out_ref, far_ref, arrived_ref, station_ref, rows_ref, jones_ref, total_ref, sent_ref,
-        far_sem, station_sem, send_sem, recv_sem, pol_send_sem, pol_recv_sem
-    ) = refs[2 * near :]
+    )(device_index.reshape(1), owners, counts, coords, windows)
+
+
+def finish_kernel(
+    half, pols, limit_ref, stations_hbm, table_ref, kept_ref, cross_ref, out_ref, pair_ref, line_ref,
+    partial_ref, station_ref, rows_ref, jones_ref, total_ref, sent_ref, station_sem, pair_send_sem,
+    pair_recv_sem, line_send_sem, line_recv_sem, pol_send_sem, pol_recv_sem
+):
     me = lax.axis_index("fs")
     pol = lax.axis_index("pol")
     capacity, _, max_blocks, lane = total_ref.shape
-    peers = [{"fs": flip(me, mask)} for mask in range(1, near)]
+    pair = {"fs": flip(me, 1)}
+    line = [{"fs": flip(me, 2 * h)} for h in range(1, half)]
     pol_peers = [{"pol": lax.rem(pol + step, pols)} for step in range(1, pols)]
-    loads = [
-        pltpu.make_async_copy(from_ref, far_ref.at[i], far_sem.at[i])
-        for i, from_ref in enumerate(far_refs)
-    ]
     stations = pltpu.make_async_copy(stations_hbm, station_ref, station_sem)
-    for load in loads:
-        load.start()
     stations.start()
     barrier = pltpu.get_barrier_semaphore()
-    for peer in peers + pol_peers:
+    for peer in [pair] + line + pol_peers:
         pl.semaphore_signal(
             barrier, inc=1, device_id=peer, device_id_type=pl.DeviceIdType.MESH
         )
-    pl.semaphore_wait(barrier, near + pols - 2)
+    pl.semaphore_wait(barrier, half + pols - 1)
+    crossing = []
+    for h in reversed(range(half)):
+        copy = pltpu.make_async_remote_copy(
+            src_ref=cross_ref.at[h],
+            dst_ref=pair_ref.at[h],
+            send_sem=pair_send_sem.at[h],
+            recv_sem=pair_recv_sem.at[h],
+            device_id=pair,
+            device_id_type=pl.DeviceIdType.MESH,
+        )
+        copy.start()
+        crossing.append(copy)
     copies = []
-    for i, peer in enumerate(peers):
+    for i, h in enumerate(reversed(range(1, half))):
+        crossing[i].wait_recv()
+        partial_ref[h - 1] = (kept_ref[h] + pair_ref[h].astype(jnp.float32)).astype(jnp.bfloat16)
         copy = pltpu.make_async_remote_copy(
-            src_ref=near_refs[i + 1],
-            dst_ref=arrived_ref.at[i],
-            send_sem=send_sem.at[i],
-            recv_sem=recv_sem.at[i],
-            device_id=peer,
+            src_ref=partial_ref.at[h - 1],
+            dst_ref=line_ref.at[h - 1],
+            send_sem=line_send_sem.at[h - 1],
+            recv_sem=line_recv_sem.at[h - 1],
+            device_id=line[h - 1],
             device_id_type=pl.DeviceIdType.MESH,
         )
         copy.start()
         copies.append(copy)
-    total = near_refs[0][...].astype(jnp.float32)
-    for i, load in enumerate(loads):
-        load.wait()
-        total = total + far_ref[i].astype(jnp.float32)
+    crossing[-1].wait_recv()
+    total_ref[...] = kept_ref[0] + pair_ref[0].astype(jnp.float32)
+    for copy in copies:
+        copy.wait_recv()
+    total = total_ref[...]
+    for h in range(1, half):
+        total = total + line_ref[h - 1].astype(jnp.float32)
     total_ref[...] = total
-    for i, copy in enumerate(copies):
-        copy.wait_recv()
-        total_ref[...] += arrived_ref[i].astype(jnp.float32)
-    sent_ref[pol] = total_ref[...].astype(jnp.bfloat16)
+    sent_ref[pol] = total.astype(jnp.bfloat16)
     pol_copies = []
     for i, peer in enumerate(pol_peers):
         copy = pltpu.make_async_remote_copy(
@@ -626,35 +627,36 @@
         return carry
 
     lax.fori_loop(0, capacity, correct, 0)
-    for copy in copies + pol_copies:
+    for copy in crossing + copies + pol_copies:
         copy.wait_send()
 
 
-def finish(limit, near_parts, far_parts, station_ids, table, pols):
-    near = len(near_parts)
-    slots = near_parts[0].shape
+def finish(limit, kept, sent, station_ids, table, pols):
+    half = kept.shape[0]
+    slots = kept.shape[1:]
     capacity, _, max_blocks, lane = slots
     smem = pl.BlockSpec(memory_space=pltpu.SMEM)
     vmem = pl.BlockSpec(memory_space=pltpu.VMEM)
     hbm = pl.BlockSpec(memory_space=pltpu.HBM)
-    anywhere = pl.BlockSpec(memory_space=pl.ANY)
     return pl.pallas_call(
-        functools.partial(finish_kernel, near, pols),
+        functools.partial(finish_kernel, half, pols),
         out_shape=jax.ShapeDtypeStruct((2, capacity, max_blocks, lane), jnp.float32),
-        in_specs=[smem, hbm, vmem] + [vmem] * near + [anywhere] * near,
+        in_specs=[smem, hbm, vmem, vmem, vmem],
         out_specs=vmem,
         scratch_shapes=[
-            pltpu.VMEM((near,) + slots, jnp.bfloat16),
-            pltpu.VMEM((near - 1,) + slots, jnp.bfloat16),
+            pltpu.VMEM((half,) + slots, jnp.bfloat16),
+            pltpu.VMEM((half - 1,) + slots, jnp.bfloat16),
+            pltpu.VMEM((half - 1,) + slots, jnp.bfloat16),
             pltpu.VMEM((capacity, 2 * max_blocks, lane), jnp.int32),
             pltpu.VMEM((table.size // lane, lane), jnp.float32),
             pltpu.VMEM((capacity, 8, max_blocks, lane), jnp.float32),
             pltpu.VMEM(slots, jnp.float32),
             pltpu.VMEM((pols,) + slots, jnp.bfloat16),
-            pltpu.SemaphoreType.DMA((near,)),
             pltpu.SemaphoreType.DMA,
-            pltpu.SemaphoreType.DMA((near - 1,)),
-            pltpu.SemaphoreType.DMA((near - 1,)),
+            pltpu.SemaphoreType.DMA((half,)),
+            pltpu.SemaphoreType.DMA((half,)),
+            pltpu.SemaphoreType.DMA((half - 1,)),
+            pltpu.SemaphoreType.DMA((half - 1,)),
             pltpu.SemaphoreType.DMA((pols - 1,)),
             pltpu.SemaphoreType.DMA((pols - 1,)),
         ],
@@ -663,10 +665,12 @@
         ),
     )(
         limit,
-        station_ids.reshape(capacity, 2 * max_blocks, lane),
+        pltpu.with_memory_space_constraint(
+            station_ids.reshape(capacity, 2 * max_blocks, lane), pltpu.HBM
+        ),
         table,
-        *near_parts,
-        *far_parts,
+        kept,
+        sent,
     )
 
 
@@ -674,16 +678,10 @@
     device_index = lax.axis_index("fs").astype(jnp.int32)
     device_count, pols = lax.axis_size("fs"), lax.axis_size("pol")
     windows, all_coords = transform(facets[0], coords, device_count)
-    near = device_count // 2
-    first, parts = predict(windows, owners, counts, all_coords, device_index, facets.shape[1])
-    far_parts = [
-        lax.ppermute(part, "fs", [(i, i ^ (near + mask)) for i in range(device_count)])
-        for mask, part in enumerate(parts)
-    ]
-    limit, near_parts = predict(
-        windows, owners, counts, all_coords, device_index, facets.shape[1], (first,)
+    limit, kept, sent = predict(
+        windows, owners, counts, all_coords, device_index, facets.shape[1]
     )
-    return finish(limit, near_parts, far_parts, station_ids, jones_table, pols)[None]
+    return finish(limit, kept, sent, station_ids, jones_table, pols)[None]
 
 
 def solution(mesh):

time: 72.1 us -> 60.9 us (0.84); the launches traced: 73.5 us -> 61 us
  starting transfers between devices: 18.2 us -> 0 us
  Pallas kernels: 54.5 us -> 60.3 us
    ppermute x4 -> x0, starting transfers between devices: 18.2 us -> none  [on_device(): lax.ppermute(part, 'fs', [(i, i ^ near + mask) for i in range(device_coun...]
    pallas_call x3 -> x2, Pallas kernels: 35.6 us -> 39.1 us  [the longest x1 21.1 us: predict(): pl.pallas_call(functools.partial(predict_kernel, facet_local, device_coun...]
    pallas_call x1, Pallas kernels: 18.9 us -> 21.2 us  [transform(): pl.pallas_call(functools.partial(transform_kernel, device_count), out_sha...]
  transfers between devices with their start and end apart: 4 -> 0, of which waited for: 0 -> 0; matrix products, arithmetic and copies ran while one was open for 0% -> 0% of each run, Pallas kernels for 24% -> 0%
where the time goes in v3:
time: 60.9 us; the launch traced here: 61 us
  Pallas kernels  60.3 us (99%)
  local copies, waits for them, and re-layouts  0.67 us (1%)
    pallas_call x1, Pallas kernels, transform(): pl.pallas_call(functools.partial(transform_kernel, device_count), out_sha...  21.2 us
    pallas_call x1, Pallas kernels, predict(): pl.pallas_call(functools.partial(predict_kernel, facet_local, device_coun...  21.1 us
    pallas_call x1, Pallas kernels, finish(): pl.pallas_call(functools.partial(finish_kernel, half, pols), out_shape=ja...  18 us

profile of v3, /device:TPU:1, one launch (start us, length us, event | category | flops | bytes accessed | tf_op | source)
XLA Modules:
  0.0 61.0 jit_solution(18265812376181126386)
XLA Ops:
  0.0 0.0 copy-start.1
  0.0 0.0 copy-start.2
  0.0 21.2 %shard_map.73 = (bf16[64,256,256]{2,1,0:T(8,128)(2,1)S(1)}, f32[8,2,16,8,128]{4,3,2,1,0:T(8,128)S(1)}) custom-call(bf16[8,4096,128]{2,1,0:T(8,128)(2,1)} %bitcast.6, bf16[69,128,128]{2,1,0:T(8,128)(2,1)} %constant.8.clone.tables_hbm, f32[2,16,8,128]{3,2,1,0:T(8,128)} %coords_ref.1), custom_call_target="tpu_custom_call" | custom-call | flops 5000000000 | bytes 16777216 | tf_op jit(solution)/shard_map/pallas_call | solution.py:314
  21.2 0.0 copy-done.1
  21.2 0.0 copy-done.2
  21.2 0.0 copy-start
  21.2 21.1 %shard_map.74 = (s32[16]{0:T(128)S(1)}, f32[4,16,2,8,128]{4,3,2,1,0:T(8,128)S(1)}, bf16[4,16,2,8,128]{4,3,2,1,0:T(8,128)(2,1)S(1)}) custom-call(s32[1]{0:T(128)} %bitcast.index_ref, s32[64]{0:T(128)S(1)} %copy-done.1, s32[64]{0:T(128)S(1)} %copy-done.2, f32[8,2,16,8,128]{4,3,2,1,0:T(8,128)S(1)} %get-tuple-element.10.coords_ref, ...), custom_call_target="tpu_custom_call" | custom-call | flops 20000000000 | bytes 1048576 | tf_op jit(solution)/shard_map/pallas_call | solution.py:484
  42.4 0.0 copy-done
  42.4 18.0 %shard_map.75 = f32[2,16,8,128]{3,2,1,0:T(8,128)S(1)} custom-call(s32[16]{0:T(128)S(1)} %get-tuple-element.12.limit_ref, s32[16,16,128]{2,1,0:T(8,128)} %bitcast.5, f32[8,512]{1,0:T(8,128)S(1)} %copy-done, f32[4,16,2,8,128]{4,3,2,1,0:T(8,128)S(1)} %get-tuple-element.13.kept_ref, bf16[4,16,2,8,128]{4,3,2,1,0:T(8,128)(2,1)S(1)} %get-tuple-element.14.cross_ref), custom_call_target="tpu_custom_call" | custom-call | tf_op jit(solution)/shard_map/pallas_call | solution.py:641
  60.4 0.7 %copy.9 = f32[1,2,16,8,128]{4,3,2,1,0:T(8,128)} copy(f32[1,2,16,8,128]{4,3,2,1,0:T(8,128)S(1)} %bitcast.4) | data formatting | bytes 262144
Async XLA Ops:
  0.0 21.2 %copy-start.1 = (s32[64]{0:T(128)S(1)}, s32[64]{0:T(128)}, u32[]{:S(2)}) copy-start(s32[64]{0:T(128)} %owners_ref.1) | copy-start | bytes 772
  0.0 21.2 %copy-start.2 = (s32[64]{0:T(128)S(1)}, s32[64]{0:T(128)}, u32[]{:S(2)}) copy-start(s32[64]{0:T(128)} %counts_ref.1) | copy-start | bytes 772
  21.2 21.1 %copy-start = (f32[8,512]{1,0:T(8,128)S(1)}, f32[8,512]{1,0:T(8,128)}, u32[]{:S(2)}) copy-start(f32[8,512]{1,0:T(8,128)} %table_ref.1) | copy-start | bytes 49156

commit v4 on v3

--- a/solution.py
+++ b/solution.py
@@ -19,7 +19,7 @@
 PITCH = 65
 CHUNK = 2048
 UNROLL = 32
-PAIRS = 4
+PAIRS = 3
 VMEM_BYTES = 67043328
 SLACK = 13000 * 1024
 
@@ -125,7 +125,7 @@
 def transform_kernel(
     device_count, strips_ref, tables_hbm, coords_ref, out_ref, gathered_ref,
     strip_ref, first_ref, mix_ref, second_ref, mixed_ref, turned_ref, everyone_ref, strip_sem, table_sem, own_sem,
-    pair_send_sem, pair_recv_sem, line_send_sem, line_recv_sem, core_send_sem, core_recv_sem
+    fs_send_sem, fs_recv_sem, core_send_sem, core_recv_sem
 ):
     me = lax.axis_index("fs")
     pol = lax.axis_index("pol")
@@ -165,14 +165,10 @@
             tables[1].start()
             tables[2].start()
 
-    across = {"fs": flip(me, 1)}
-    line = {h: {"fs": flip(me, 2 * h)} for h in range(1, device_count // 2)}
+    peers = [{"fs": flip(me, mask)} for mask in range(1, device_count)]
     barrier = pltpu.get_barrier_semaphore()
-    for peer in [partner, across] + list(line.values()):
+    for peer in [partner] + peers:
         pl.semaphore_signal(barrier, inc=1, device_id=peer, device_id_type=pl.DeviceIdType.MESH)
-    pl.semaphore_wait(barrier, device_count // 2 + 1)
-    own.wait()
-    sends = []
 
     def send(source, peer, send_sem, recv_sem, index):
         piece = everyone_ref.at[source, :, pl.ds(half * slots, slots)]
@@ -185,23 +181,15 @@
             device_id_type=pl.DeviceIdType.MESH,
         )
         copy.start()
-        sends.append(copy)
         return copy
 
-    def to_partner(mask):
-        return send(flip(me, mask), partner, core_send_sem, core_recv_sem, mask - 1)
-
-    crossed = {0: send(me, across, pair_send_sem, pair_recv_sem, 0)}
-    reached = {
-        h: send(me, line[h], line_send_sem, line_recv_sem, h - 1) for h in reversed(list(line))
-    }
+    sends = {}
     handed = []
 
-    def relay(masks):
-        for h in masks:
-            reached[h].wait_recv()
-            crossed[h] = send(flip(me, 2 * h), across, pair_send_sem, pair_recv_sem, h)
-            handed.append(to_partner(2 * h))
+    def hand_on(masks):
+        for mask in masks:
+            sends[mask].wait_recv()
+            handed.append(send(flip(me, mask), partner, core_send_sem, core_recv_sem, mask - 1))
 
     tables[0].wait()
     mix = jnp.concatenate(
@@ -233,6 +221,11 @@
                 return carry
 
             lax.fori_loop(0, FH // CHUNK, join, 0)
+            if group == 0 and pair == 0:
+                pl.semaphore_wait(barrier, device_count)
+                own.wait()
+                for mask in reversed(range(1, device_count)):
+                    sends[mask] = send(me, peers[mask - 1], fs_send_sem, fs_recv_sem, mask - 1)
         if group == 0:
             tables[1].wait()
             tables[2].wait()
@@ -265,8 +258,6 @@
             return carry
 
         lax.fori_loop(0, S // UNROLL, first, 0)
-        if group == 0:
-            relay([1])
 
         def second(i, carry):
             for u in range(UNROLL):
@@ -283,8 +274,8 @@
             return carry
 
         lax.fori_loop(0, W // UNROLL, second, 0)
-        if group == 0:
-            relay(range(2, device_count // 2))
+        if group == facet_local // span - 1:
+            hand_on(range(1, device_count // 2))
 
         def third(i, carry, group=group):
             for u in range(2):
@@ -294,12 +285,10 @@
 
         lax.fori_loop(0, S // 2, third, 0)
 
-    for h in range(device_count // 2):
-        crossed[h].wait_recv()
-        handed.append(to_partner(2 * h + 1))
+    hand_on(range(device_count // 2, device_count))
     for copy in handed:
         copy.wait_recv()
-    for copy in sends:
+    for copy in list(sends.values()) + handed:
         copy.wait_send()
     gathered_ref[...] = everyone_ref[...]
 
@@ -330,10 +319,8 @@
             pltpu.SemaphoreType.DMA((facet_local,)),
             pltpu.SemaphoreType.DMA((3,)),
             pltpu.SemaphoreType.DMA,
-            pltpu.SemaphoreType.DMA((device_count // 2,)),
-            pltpu.SemaphoreType.DMA((device_count // 2,)),
-            pltpu.SemaphoreType.DMA((device_count // 2 - 1,)),
-            pltpu.SemaphoreType.DMA((device_count // 2 - 1,)),
+            pltpu.SemaphoreType.DMA((device_count - 1,)),
+            pltpu.SemaphoreType.DMA((device_count - 1,)),
             pltpu.SemaphoreType.DMA((device_count - 1,)),
             pltpu.SemaphoreType.DMA((device_count - 1,)),
         ],
@@ -352,12 +339,12 @@
 
 def predict_kernel(
     facet_local, device_count, index_ref, owners_ref, counts_ref, coords_ref, windows_ref,
-    limit_ref, kept_ref, sent_ref, out_ref, table_ref, row_ref, place_ref, load_ref, loads_ref
+    limit_ref, kept_ref, sent_ref, out_ref, table_0_ref, table_1_ref, row_0_ref,
+    row_1_ref, place_ref, load_ref, loads_ref
 ):
     lane = out_ref.shape[3]
-    half = device_count // 2
     subgrids = owners_ref.shape[0]
-    capacity = kept_ref.shape[1]
+    capacity = kept_ref.shape[0]
     span = min(SPAN, facet_local)
     groups = facet_local // span
     steps = span // 2
@@ -367,9 +354,11 @@
     col_middle = (lax.rem(first, R) * W).astype(jnp.float32) + (0.5 * (span * W - 1) - SG // 2)
     ramp = lax.broadcasted_iota(jnp.int32, (8, lane), 0).astype(jnp.float32)
     fine = (ramp + 0.5) * unit
-    col_pick = jnp.where(ramp == 1.0, 0.0, col_middle + (ramp - 2.0) * (span * W))
-    col_pick = jnp.where(ramp == 0.0, 8.0, col_pick) * unit
-    row_pick = jnp.where(ramp == 0.0, 0.0, jnp.where(ramp == 1.0, 8.0, row_middle)) * unit
+    second = ramp >= 4.0
+    kind = jnp.where(second, ramp - 4.0, ramp)
+    col_pick = jnp.where(kind == 1.0, 0.0, col_middle + (kind - 2.0) * (span * W))
+    col_pick = jnp.where(kind == 0.0, 8.0, col_pick) * unit
+    row_pick = jnp.where(kind == 0.0, 0.0, jnp.where(kind == 1.0, 8.0, row_middle)) * unit
     out_ref[...] = jnp.zeros_like(out_ref)
 
     def clear(ref):
@@ -390,7 +379,7 @@
         count = counts_ref[s]
         offset = owner ^ me
         load_ref[s] = load
-        place_ref[s] = ((offset & 1) * half + (offset >> 1)) * capacity + load
+        place_ref[s] = offset * capacity + load
 
         @pl.when(owner == me)
         def _():
@@ -410,30 +399,31 @@
             s = jnp.where(done, jnp.minimum(s + 1, subgrids - 1), s)
         return items, (s, b)
 
-    def tables(u, turn, s, b):
+    def tables(u, refs, s, b):
+        table_ref, row_ref = refs
         owner, load = owners_ref[s], load_ref[s]
+        at = [[coords_ref[owner, axis, load, pl.ds(b + h, 1), :] for h in range(2)] for axis in range(2)]
+        x, y = [jnp.where(second, one[1], one[0]) for one in at]
+        picked = phase(x * row_pick + y * col_pick)
+        row_ref[u, 2, :16] = jnp.concatenate(picked, axis=0)
         for h in range(2):
-            x = coords_ref[owner, 0, load, pl.ds(b + h, 1), :]
-            y = coords_ref[owner, 1, load, pl.ds(b + h, 1), :]
-            picked = phase(x * row_pick + y * col_pick)
             col_step, row_step = [
-                [jnp.broadcast_to(part[i : i + 1], (8, lane)) for part in picked] for i in range(2)
+                [jnp.broadcast_to(part[4 * h + i : 4 * h + i + 1], (8, lane)) for part in picked]
+                for i in range(2)
             ]
-            cols = chain(phase(y * fine), col_step, steps * W // 8)
+            cols = chain(phase(at[1][h] * fine), col_step, steps * W // 8)
             entries = []
             for k in range(steps):
                 some = cols[W // 8 * k : W // 8 * (k + 1)]
                 entries += [cos for cos, _ in some] + [sin for _, sin in some]
-            table_ref[u, :, h * lane : (h + 1) * lane] = jnp.concatenate(entries, axis=0).astype(
-                jnp.bfloat16
-            )
-            rows = chain(phase(x * fine), row_step, W // 16)
-            row_ref[turn, u, h] = jnp.concatenate(
-                [cos for cos, _ in rows] + [sin for _, sin in rows] + list(picked), axis=0
-            )
-
-    def predict(u, turn, s, b):
-        grid = jnp.dot(windows_ref[s], table_ref[u], preferred_element_type=jnp.float32)
+            table_ref[u, h] = jnp.concatenate(entries, axis=0).astype(jnp.bfloat16)
+            rows = chain(phase(at[0][h] * fine), row_step, W // 16)
+            row_ref[u, h] = jnp.concatenate([cos for cos, _ in rows] + [sin for _, sin in rows], axis=0)
+
+    def predict(u, refs, s, b):
+        table_ref, row_ref = refs
+        table = jnp.concatenate([table_ref[u, 0], table_ref[u, 1]], axis=1)
+        grid = jnp.dot(windows_ref[s], table, preferred_element_type=jnp.float32)
         place = place_ref[s]
         for h in range(2):
             real = imag = None
@@ -444,12 +434,12 @@
                     for k in range(W // 8):
                         at = (2 * g + part) * W + 8 * k
                         term = grid[at : at + 8, h * lane : (h + 1) * lane] * row_ref[
-                            turn, u, h, 8 * k : 8 * k + 8, :
+                            u, h, 8 * k : 8 * k + 8, :
                         ]
                         total = term if total is None else total + term
                     sums.append(total)
-                cos = row_ref[turn, u, h, W + 2 + g : W + 3 + g, :]
-                sin = row_ref[turn, u, h, W + 10 + g : W + 11 + g, :]
+                at = 4 * h + 2 + g
+                cos, sin = row_ref[u, 2, at : at + 1, :], row_ref[u, 2, 8 + at : 9 + at, :]
                 more_real = sums[0] * cos + sums[1] * sin
                 more_imag = sums[1] * cos - sums[0] * sin
                 real = more_real if real is None else real + more_real
@@ -457,22 +447,24 @@
             out_ref[place, 0, pl.ds(b + h, 1), :] = jnp.sum(real, axis=0, keepdims=True)
             out_ref[place, 1, pl.ds(b + h, 1), :] = jnp.sum(imag, axis=0, keepdims=True)
 
+    turns = [(table_0_ref, row_0_ref), (table_1_ref, row_1_ref)]
     items, after = following(0, 0)
     for u, (s, b) in enumerate(items):
-        tables(u, 0, s, b)
+        tables(u, turns[0], s, b)
 
     def step(i, carry):
         items, after = carry
-        for u, (s, b) in enumerate(items):
-            predict(u, i & 1, s, b)
-        items, after = following(*after)
-        for u, (s, b) in enumerate(items):
-            tables(u, (i + 1) & 1, s, b)
+        for turn in range(2):
+            for u, (s, b) in enumerate(items):
+                predict(u, turns[turn], s, b)
+            items, after = following(*after)
+            for u, (s, b) in enumerate(items):
+                tables(u, turns[1 - turn], s, b)
         return items, after
 
-    lax.fori_loop(0, lax.div(total + PAIRS - 1, PAIRS), step, (items, after))
-    kept_ref[...] = out_ref[: half * capacity].reshape(kept_ref.shape)
-    sent_ref[...] = out_ref[half * capacity :].reshape(sent_ref.shape).astype(jnp.bfloat16)
+    lax.fori_loop(0, lax.div(total + 2 * PAIRS - 1, 2 * PAIRS), step, (items, after))
+    kept_ref[...] = out_ref[:capacity]
+    sent_ref[...] = out_ref[capacity:].reshape(sent_ref.shape).astype(jnp.bfloat16)
 
 
 def predict(windows, owners, counts, coords, device_index, facet_local):
@@ -480,20 +472,21 @@
     smem = pl.BlockSpec(memory_space=pltpu.SMEM)
     vmem = pl.BlockSpec(memory_space=pltpu.VMEM)
     slots = (capacity, 2, max_blocks, lane)
-    half = (device_count // 2,) + slots
     return pl.pallas_call(
         functools.partial(predict_kernel, facet_local, device_count),
         out_shape=[
             jax.ShapeDtypeStruct((capacity,), jnp.int32),
-            jax.ShapeDtypeStruct(half, jnp.float32),
-            jax.ShapeDtypeStruct(half, jnp.bfloat16),
+            jax.ShapeDtypeStruct(slots, jnp.float32),
+            jax.ShapeDtypeStruct((device_count - 1,) + slots, jnp.bfloat16),
         ],
         in_specs=[smem, smem, smem, vmem, vmem],
         out_specs=[smem, vmem, vmem],
         scratch_shapes=[
             pltpu.VMEM((device_count * capacity,) + slots[1:], jnp.float32),
-            pltpu.VMEM((PAIRS, windows.shape[2], 2 * lane), jnp.bfloat16),
-            pltpu.VMEM((2, PAIRS, 2, W + 16, lane), jnp.float32),
+            pltpu.VMEM((PAIRS, 2, windows.shape[2], lane), jnp.bfloat16),
+            pltpu.VMEM((PAIRS, 2, windows.shape[2], lane), jnp.bfloat16),
+            pltpu.VMEM((PAIRS, 3, W, lane), jnp.float32),
+            pltpu.VMEM((PAIRS, 3, W, lane), jnp.float32),
             pltpu.SMEM((owners.shape[0],), jnp.int32),
             pltpu.SMEM((owners.shape[0],), jnp.int32),
             pltpu.SMEM((device_count,), jnp.int32),
@@ -506,71 +499,38 @@
 
 
 def finish_kernel(
-    half, pols, limit_ref, stations_hbm, table_ref, kept_ref, cross_ref, out_ref, pair_ref, line_ref,
-    partial_ref, station_ref, rows_ref, jones_ref, total_ref, sent_ref, station_sem, pair_send_sem,
-    pair_recv_sem, line_send_sem, line_recv_sem, pol_send_sem, pol_recv_sem
+    parts, pols, limit_ref, stations_hbm, table_ref, kept_ref, parts_ref, out_ref, arrived_ref,
+    station_ref, rows_ref, jones_ref, total_ref, sent_ref, station_sem, send_sem, recv_sem,
+    pol_send_sem, pol_recv_sem
 ):
     me = lax.axis_index("fs")
     pol = lax.axis_index("pol")
     capacity, _, max_blocks, lane = total_ref.shape
-    pair = {"fs": flip(me, 1)}
-    line = [{"fs": flip(me, 2 * h)} for h in range(1, half)]
+    share = capacity // parts
+    peers = [{"fs": flip(me, mask)} for mask in range(1, parts_ref.shape[0] + 1)]
     pol_peers = [{"pol": lax.rem(pol + step, pols)} for step in range(1, pols)]
     stations = pltpu.make_async_copy(stations_hbm, station_ref, station_sem)
     stations.start()
     barrier = pltpu.get_barrier_semaphore()
-    for peer in [pair] + line + pol_peers:
+    for peer in peers + pol_peers:
         pl.semaphore_signal(
             barrier, inc=1, device_id=peer, device_id_type=pl.DeviceIdType.MESH
         )
-    pl.semaphore_wait(barrier, half + pols - 1)
-    crossing = []
-    for h in reversed(range(half)):
-        copy = pltpu.make_async_remote_copy(
-            src_ref=cross_ref.at[h],
-            dst_ref=pair_ref.at[h],
-            send_sem=pair_send_sem.at[h],
-            recv_sem=pair_recv_sem.at[h],
-            device_id=pair,
-            device_id_type=pl.DeviceIdType.MESH,
-        )
-        copy.start()
-        crossing.append(copy)
+    pl.semaphore_wait(barrier, len(peers) + len(pol_peers))
     copies = []
-    for i, h in enumerate(reversed(range(1, half))):
-        crossing[i].wait_recv()
-        partial_ref[h - 1] = (kept_ref[h] + pair_ref[h].astype(jnp.float32)).astype(jnp.bfloat16)
-        copy = pltpu.make_async_remote_copy(
-            src_ref=partial_ref.at[h - 1],
-            dst_ref=line_ref.at[h - 1],
-            send_sem=line_send_sem.at[h - 1],
-            recv_sem=line_recv_sem.at[h - 1],
-            device_id=line[h - 1],
-            device_id_type=pl.DeviceIdType.MESH,
-        )
-        copy.start()
-        copies.append(copy)
-    crossing[-1].wait_recv()
-    total_ref[...] = kept_ref[0] + pair_ref[0].astype(jnp.float32)
-    for copy in copies:
-        copy.wait_recv()
-    total = total_ref[...]
-    for h in range(1, half):
-        total = total + line_ref[h - 1].astype(jnp.float32)
-    total_ref[...] = total
-    sent_ref[pol] = total.astype(jnp.bfloat16)
-    pol_copies = []
-    for i, peer in enumerate(pol_peers):
-        copy = pltpu.make_async_remote_copy(
-            src_ref=sent_ref.at[pol],
-            dst_ref=sent_ref.at[pol],
-            send_sem=pol_send_sem.at[i],
-            recv_sem=pol_recv_sem.at[i],
-            device_id=peer,
-            device_id_type=pl.DeviceIdType.MESH,
-        )
-        copy.start()
-        pol_copies.append(copy)
+    for part in range(parts):
+        slots = pl.ds(part * share, share)
+        for i, peer in reversed(list(enumerate(peers))):
+            copy = pltpu.make_async_remote_copy(
+                src_ref=parts_ref.at[i, slots],
+                dst_ref=arrived_ref.at[i, slots],
+                send_sem=send_sem.at[part, i],
+                recv_sem=recv_sem.at[part, i],
+                device_id=peer,
+                device_id_type=pl.DeviceIdType.MESH,
+            )
+            copy.start()
+            copies.append(copy)
     stations.wait()
     chunks = table_ref.shape[1] // lane
     firsts = [4 * lax.div(pol, 2), 4 * lax.rem(pol, 2)]
@@ -597,8 +557,26 @@
         return carry
 
     lax.fori_loop(0, capacity, look_up, 0)
-    for copy in pol_copies:
-        copy.wait_recv()
+    pol_copies = []
+    for part in range(parts):
+        slots = pl.ds(part * share, share)
+        total = kept_ref[slots]
+        for i in range(len(peers)):
+            copies[part * len(peers) + len(peers) - 1 - i].wait_recv()
+            total = total + arrived_ref[i, slots].astype(jnp.float32)
+        total_ref[slots] = total
+        sent_ref[pol, slots] = total.astype(jnp.bfloat16)
+        for i, peer in enumerate(pol_peers):
+            copy = pltpu.make_async_remote_copy(
+                src_ref=sent_ref.at[pol, slots],
+                dst_ref=sent_ref.at[pol, slots],
+                send_sem=pol_send_sem.at[part, i],
+                recv_sem=pol_recv_sem.at[part, i],
+                device_id=peer,
+                device_id_type=pl.DeviceIdType.MESH,
+            )
+            copy.start()
+            pol_copies.append(copy)
     block = lax.broadcasted_iota(jnp.int32, (max_blocks, lane), 0)
 
     def product(a, b):
@@ -626,39 +604,39 @@
         out_ref[1, load] = jnp.where(keep, imag, 0.0)
         return carry
 
-    lax.fori_loop(0, capacity, correct, 0)
-    for copy in crossing + copies + pol_copies:
+    for part in range(parts):
+        for copy in pol_copies[part * len(pol_peers) : (part + 1) * len(pol_peers)]:
+            copy.wait_recv()
+        lax.fori_loop(part * share, (part + 1) * share, correct, 0)
+    for copy in copies + pol_copies:
         copy.wait_send()
 
 
 def finish(limit, kept, sent, station_ids, table, pols):
-    half = kept.shape[0]
-    slots = kept.shape[1:]
+    peers = sent.shape[0]
+    slots = kept.shape
     capacity, _, max_blocks, lane = slots
+    parts = max(1, min(capacity, 32 // (peers + 1)))
     smem = pl.BlockSpec(memory_space=pltpu.SMEM)
     vmem = pl.BlockSpec(memory_space=pltpu.VMEM)
     hbm = pl.BlockSpec(memory_space=pltpu.HBM)
     return pl.pallas_call(
-        functools.partial(finish_kernel, half, pols),
+        functools.partial(finish_kernel, parts, pols),
         out_shape=jax.ShapeDtypeStruct((2, capacity, max_blocks, lane), jnp.float32),
         in_specs=[smem, hbm, vmem, vmem, vmem],
         out_specs=vmem,
         scratch_shapes=[
-            pltpu.VMEM((half,) + slots, jnp.bfloat16),
-            pltpu.VMEM((half - 1,) + slots, jnp.bfloat16),
-            pltpu.VMEM((half - 1,) + slots, jnp.bfloat16),
+            pltpu.VMEM((peers,) + slots, jnp.bfloat16),
             pltpu.VMEM((capacity, 2 * max_blocks, lane), jnp.int32),
             pltpu.VMEM((table.size // lane, lane), jnp.float32),
             pltpu.VMEM((capacity, 8, max_blocks, lane), jnp.float32),
             pltpu.VMEM(slots, jnp.float32),
             pltpu.VMEM((pols,) + slots, jnp.bfloat16),
             pltpu.SemaphoreType.DMA,
-            pltpu.SemaphoreType.DMA((half,)),
-            pltpu.SemaphoreType.DMA((half,)),
-            pltpu.SemaphoreType.DMA((half - 1,)),
-            pltpu.SemaphoreType.DMA((half - 1,)),
-            pltpu.SemaphoreType.DMA((pols - 1,)),
-            pltpu.SemaphoreType.DMA((pols - 1,)),
+            pltpu.SemaphoreType.DMA((parts, peers)),
+            pltpu.SemaphoreType.DMA((parts, peers)),
+            pltpu.SemaphoreType.DMA((parts, pols - 1)),
+            pltpu.SemaphoreType.DMA((parts, pols - 1)),
         ],
         compiler_params=pltpu.CompilerParams(
             vmem_limit_bytes=8 * 2**20, collective_id=1, has_side_effects=True

time: 60.9 us -> 60.5 us (level); the launches traced: 61 us -> 60 us
  Pallas kernels: 60.3 us -> 59.3 us
    pallas_call x1, Pallas kernels: 21.1 us -> 17.6 us  [predict(): pl.pallas_call(functools.partial(predict_kernel, facet_local, device_coun...]
    pallas_call x1, Pallas kernels: 18 us -> 20.4 us  [finish(): pl.pallas_call(functools.partial(finish_kernel, parts, pols), out_shape=j...]
where the time goes in v4:
time: 60.5 us; the launch traced here: 60 us
  Pallas kernels  59.3 us (98%)
  local copies, waits for them, and re-layouts  0.67 us (1%)
    pallas_call x1, Pallas kernels, transform(): pl.pallas_call(functools.partial(transform_kernel, device_count), out_sha...  21.4 us
    pallas_call x1, Pallas kernels, finish(): pl.pallas_call(functools.partial(finish_kernel, parts, pols), out_shape=j...  20.4 us
    pallas_call x1, Pallas kernels, predict(): pl.pallas_call(functools.partial(predict_kernel, facet_local, device_coun...  17.6 us

profile of v4, /device:TPU:1, one launch (start us, length us, event | category | flops | bytes accessed | tf_op | source)
XLA Modules:
  0.0 60.0 jit_solution(5473435719346694762)
XLA Ops:
  0.0 0.0 copy-start.1
  0.0 0.0 copy-start.2
  0.0 21.4 %shard_map.73 = (bf16[64,256,256]{2,1,0:T(8,128)(2,1)S(1)}, f32[8,2,16,8,128]{4,3,2,1,0:T(8,128)S(1)}) custom-call(bf16[8,4096,128]{2,1,0:T(8,128)(2,1)} %bitcast.6, bf16[69,128,128]{2,1,0:T(8,128)(2,1)} %constant.8.clone.tables_hbm, f32[2,16,8,128]{3,2,1,0:T(8,128)} %coords_ref.1), custom_call_target="tpu_custom_call" | custom-call | flops 5000000000 | bytes 16777216 | tf_op jit(solution)/shard_map/pallas_call | solution.py:303
  21.4 0.0 copy-done.1
  21.4 0.0 copy-done.2
  21.4 0.0 copy-start
  21.4 17.6 %shard_map.74 = (s32[16]{0:T(128)S(1)}, f32[16,2,8,128]{3,2,1,0:T(8,128)S(1)}, bf16[7,16,2,8,128]{4,3,2,1,0:T(8,128)(2,1)S(1)}) custom-call(s32[1]{0:T(128)} %bitcast.index_ref, s32[64]{0:T(128)S(1)} %copy-done.1, s32[64]{0:T(128)S(1)} %copy-done.2, f32[8,2,16,8,128]{4,3,2,1,0:T(8,128)S(1)} %get-tuple-element.10.coords_ref, ...), custom_call_target="tpu_custom_call" | custom-call | flops 20000000000 | bytes 1048576 | tf_op jit(solution)/shard_map/pallas_call | solution.py:475
  39.0 0.0 copy-done
  39.0 20.4 %shard_map.75 = f32[2,16,8,128]{3,2,1,0:T(8,128)S(1)} custom-call(s32[16]{0:T(128)S(1)} %get-tuple-element.12.limit_ref, s32[16,16,128]{2,1,0:T(8,128)} %bitcast.5, f32[8,512]{1,0:T(8,128)S(1)} %copy-done, f32[16,2,8,128]{3,2,1,0:T(8,128)S(1)} %get-tuple-element.13.kept_ref, bf16[7,16,2,8,128]{4,3,2,1,0:T(8,128)(2,1)S(1)} %get-tuple-element.14.parts_ref), custom_call_target="tpu_custom_call" | custom-call | tf_op jit(solution)/shard_map/pallas_call | solution.py:623
  59.4 0.7 %copy.9 = f32[1,2,16,8,128]{4,3,2,1,0:T(8,128)} copy(f32[1,2,16,8,128]{4,3,2,1,0:T(8,128)S(1)} %bitcast.4) | data formatting | bytes 262144
Async XLA Ops:
  0.0 21.4 %copy-start.1 = (s32[64]{0:T(128)S(1)}, s32[64]{0:T(128)}, u32[]{:S(2)}) copy-start(s32[64]{0:T(128)} %owners_ref.1) | copy-start | bytes 772
  0.0 21.4 %copy-start.2 = (s32[64]{0:T(128)S(1)}, s32[64]{0:T(128)}, u32[]{:S(2)}) copy-start(s32[64]{0:T(128)} %counts_ref.1) | copy-start | bytes 772
  21.4 17.6 %copy-start = (f32[8,512]{1,0:T(8,128)S(1)}, f32[8,512]{1,0:T(8,128)}, u32[]{:S(2)}) copy-start(f32[8,512]{1,0:T(8,128)} %table_ref.1) | copy-start | bytes 49156
